TPU v7x, 32 devices: a whole 2x2x4 slice. The times are simulated.
32 devices in a mesh: rep: 2 (over y), seq: 4 (over x, core), head: 4 (over z).
Axes of the slice: x: 2, y: 2, z: 4, core: 2. Of those that a mesh axis runs over, the one named last changes fastest.
Arguments:
- query: bfloat16 [32768, 2048], P(('rep', 'seq', 'head')), parts along dimension 0, may hold values from -6 to 6
- key: bfloat16 [32768, 2048], P(('rep', 'seq', 'head')), parts along dimension 0, may hold values from -6 to 6
- value: bfloat16 [32768, 2048], P(('rep', 'seq', 'head')), parts along dimension 0, may hold values from -6 to 6
- grad_out: bfloat16 [32768, 2048], P(('rep', 'seq', 'head')), parts along dimension 0, may hold values from -6 to 6
- level_weights: bfloat16 [32768, 128], P(('rep', 'seq', 'head')), parts along dimension 0, may hold values from 0.25 to 4
Outputs:
- attended: bfloat16 [32768, 2048], P(('rep', 'seq', 'head')), parts along dimension 0
- grad_query: bfloat16 [32768, 2048], P(('rep', 'seq', 'head')), parts along dimension 0
- grad_key: bfloat16 [32768, 2048], P(('rep', 'seq', 'head')), parts along dimension 0
- grad_value: bfloat16 [32768, 2048], P(('rep', 'seq', 'head')), parts along dimension 0
- grad_weights: bfloat16 [32768, 128], P(('rep', 'seq', 'head')), parts along dimension 0
There are 2 independent parts, one for each index of `rep`. A program takes and returns all parts, laid end to end along the dimension named above; each array names one. Nothing has to cross between parts.
All inputs are finite; a program needn't handle non-finite values.
Results may differ from a plain program's by a relative error of at most 0.0056.
Values may be sent and summed in bfloat16 or wider, within the bound.
A program may use at most 384 MiB of HBM per device.

v0:
```python
import math

import jax
import jax.numpy as jnp
from jax import lax
from jax.sharding import PartitionSpec as P

DH = 128
C = 128
LEVELS = 8


def level_scale(level):
    if level == 0:
        return 1.0 / math.sqrt(DH * C)
    return 1.0 / math.sqrt(DH * C * 2 ** (level - 1))


def bucket_matrix(count, level_bit):
    rows = jnp.arange(count, dtype=jnp.int32)[:, None]
    columns = jnp.arange(count, dtype=jnp.int32)[None, :]
    stride = 2**level_bit
    reading = rows // stride % 2 == 1
    inside = columns // stride == rows // (2 * stride) * 2
    return jnp.where(reading & inside, 1.0, 0.0).astype(jnp.float32)


def local_part(query, key, value, grad_out, level_weights):
    heads = query.shape[1] // DH
    stretches = query.shape[0] // C
    blocks = (stretches, C, heads, DH)
    query_blocks = query.reshape(blocks)
    key_blocks = key.reshape(blocks)
    value_blocks = value.reshape(blocks)
    grad_blocks = grad_out.reshape(blocks)
    weights = level_weights.reshape(stretches, C, heads, LEVELS).astype(jnp.float32)
    mask = jnp.tril(jnp.ones((C, C), jnp.float32))
    scores = jnp.einsum(
        "ntgd,nsgd->ngts", query_blocks, key_blocks, preferred_element_type=jnp.float32
    ) * (level_scale(0) * mask)
    first = jnp.transpose(weights[..., 0], (0, 2, 1))[..., None]
    probs = (first * scores).astype(jnp.bfloat16)
    attended = jnp.einsum(
        "ngts,nsgd->ntgd", probs, value_blocks, preferred_element_type=jnp.float32
    )
    grad_probs = jnp.einsum(
        "ntge,nsge->ngts", grad_blocks, value_blocks, preferred_element_type=jnp.float32
    )
    grad_levels = [jnp.transpose(jnp.sum(scores * grad_probs, axis=-1), (0, 2, 1))]
    grad_scores = (first * grad_probs * (level_scale(0) * mask)).astype(jnp.bfloat16)
    grad_query = jnp.einsum(
        "ngts,nsgd->ntgd", grad_scores, key_blocks, preferred_element_type=jnp.float32
    )
    grad_key = jnp.einsum(
        "ngts,ntgd->nsgd", grad_scores, query_blocks, preferred_element_type=jnp.float32
    )
    grad_value = jnp.einsum(
        "ngts,ntge->nsge", probs, grad_blocks, preferred_element_type=jnp.float32
    )
    states = jnp.einsum(
        "nsgd,nsge->ngde", key_blocks, value_blocks, preferred_element_type=jnp.float32
    )
    products = []
    for level in range(1, LEVELS):
        weighted = (weights[..., level : level + 1] * query_blocks).astype(jnp.bfloat16)
        products.append(
            jnp.einsum("ntgd,ntge->ngde", weighted, grad_blocks, preferred_element_type=jnp.float32)
        )
    blocks_all = (query_blocks, key_blocks, value_blocks, grad_blocks, weights)
    partial_value = (attended, grad_levels, grad_query, grad_key, grad_value)
    return (blocks_all, partial_value, states, products)


def finish(blocks_all, partial_value, states, products, cross_reads, cross_adjoint):
    query_blocks, key_blocks, value_blocks, grad_blocks, weights = blocks_all
    attended, grad_levels, grad_query, grad_key, grad_value = partial_value
    stretches = query_blocks.shape[0]
    heads = query_blocks.shape[2]
    local_bits = stretches.bit_length() - 1
    adjoint = jnp.zeros((stretches, heads, DH, DH), jnp.float32)
    for level in range(1, LEVELS):
        factor = level_scale(level)
        if level <= local_bits:
            mapping = bucket_matrix(stretches, level - 1)
            summed = jnp.einsum("ij,jgde->igde", mapping, states, precision=lax.Precision.HIGHEST)
            read_state = (factor * summed).astype(jnp.bfloat16)
            reads = jnp.einsum(
                "ntgd,ngde->ntge", query_blocks, read_state, preferred_element_type=jnp.float32
            )
            backward = jnp.einsum(
                "ntge,ngde->ntgd", grad_blocks, read_state, preferred_element_type=jnp.float32
            )
            adjoint = adjoint + factor * jnp.einsum(
                "ij,igde->jgde", mapping, products[level - 1], precision=lax.Precision.HIGHEST
            )
        else:
            index = level - 1 - local_bits
            read_state = (factor * cross_reads[index]).astype(jnp.bfloat16)
            reads = jnp.einsum(
                "ntgd,gde->ntge", query_blocks, read_state, preferred_element_type=jnp.float32
            )
            backward = jnp.einsum(
                "ntge,gde->ntgd", grad_blocks, read_state, preferred_element_type=jnp.float32
            )
            adjoint = adjoint + factor * cross_adjoint[index][None]
        weight = weights[..., level : level + 1]
        attended = attended + weight * reads
        grad_levels.append(jnp.sum(grad_blocks.astype(jnp.float32) * reads, axis=-1))
        grad_query = grad_query + weight * backward
    adjoint_low = adjoint.astype(jnp.bfloat16)
    grad_key = grad_key + jnp.einsum(
        "nsge,ngde->nsgd", value_blocks, adjoint_low, preferred_element_type=jnp.float32
    )
    grad_value = grad_value + jnp.einsum(
        "nsgd,ngde->nsge", key_blocks, adjoint_low, preferred_element_type=jnp.float32
    )

    def flatten(array, width):
        return array.reshape(stretches * C, heads * width).astype(jnp.bfloat16)

    return (
        flatten(attended, DH),
        flatten(grad_query, DH),
        flatten(grad_key, DH),
        flatten(grad_value, DH),
        flatten(jnp.stack(grad_levels, axis=-1), LEVELS),
    )


def cross_inputs(states, products, stretches, cross_bits):
    local_bits = stretches.bit_length() - 1
    cross_total = jnp.sum(states, axis=0)
    cross_products = jnp.stack(
        [jnp.sum(products[local_bits + level_bit], axis=0) for level_bit in range(cross_bits)]
    )
    return (cross_total, cross_products)


def shards(query, key, value, grad_out, level_weights):
    query, key, value, grad_out, level_weights = (
        lax.all_to_all(query, "head", split_axis=1, concat_axis=0, tiled=True),
        lax.all_to_all(key, "head", split_axis=1, concat_axis=0, tiled=True),
        lax.all_to_all(value, "head", split_axis=1, concat_axis=0, tiled=True),
        lax.all_to_all(grad_out, "head", split_axis=1, concat_axis=0, tiled=True),
        lax.all_to_all(level_weights, "head", split_axis=1, concat_axis=0, tiled=True),
    )
    blocks_all, partial_value, states, products = local_part(
        query, key, value, grad_out, level_weights
    )
    stretches = states.shape[0]
    cross_bits = lax.axis_size("seq").bit_length() - 1
    position = lax.axis_index("seq")
    cross_total, cross_products = cross_inputs(states, products, stretches, cross_bits)
    totals = lax.all_gather(cross_total[None], "seq", axis=0, tiled=True)
    sums = lax.all_gather(cross_products[None], "seq", axis=0, tiled=True)
    count = totals.shape[0]
    source = jnp.arange(count, dtype=jnp.int32)[:, None]
    powers = (2 ** jnp.arange(cross_bits, dtype=jnp.int32))[None, :]
    base = position // (2 * powers) * (2 * powers)
    owned = position // powers % 2
    lower = (source >= base) & (source < base + powers)
    upper = (source >= base + powers) & (source < base + 2 * powers)
    forward = jnp.where(lower & (owned == 1), 1.0, 0.0).astype(jnp.float32)
    backward = jnp.where(upper & (owned == 0), 1.0, 0.0).astype(jnp.float32)
    read_sum = jnp.einsum("qb,qgde->bgde", forward, totals, precision=lax.Precision.HIGHEST)
    adjoint_sum = jnp.einsum("qb,qbgde->bgde", backward, sums, precision=lax.Precision.HIGHEST)
    results = finish(blocks_all, partial_value, states, products, read_sum, adjoint_sum)
    return (
        lax.all_to_all(results[0], "head", split_axis=0, concat_axis=1, tiled=True),
        lax.all_to_all(results[1], "head", split_axis=0, concat_axis=1, tiled=True),
        lax.all_to_all(results[2], "head", split_axis=0, concat_axis=1, tiled=True),
        lax.all_to_all(results[3], "head", split_axis=0, concat_axis=1, tiled=True),
        lax.all_to_all(results[4], "head", split_axis=0, concat_axis=1, tiled=True),
    )


def solution(mesh):
    return jax.shard_map(
        shards,
        mesh=mesh,
        in_specs=(
            P(("rep", "seq", "head"), None),
            P(("rep", "seq", "head"), None),
            P(("rep", "seq", "head"), None),
            P(("rep", "seq", "head"), None),
            P(("rep", "seq", "head"), None),
        ),
        out_specs=(
            P(("rep", "seq", "head"), None),
            P(("rep", "seq", "head"), None),
            P(("rep", "seq", "head"), None),
            P(("rep", "seq", "head"), None),
            P(("rep", "seq", "head"), None),
        ),
        check_vma=False,
    )
```

profile of v0, /device:TPU:3, one launch (start us, length us, event | category | flops | bytes accessed | tf_op | source)
XLA Modules:
  0.0 1142.9 jit_solution(13611935831016947654)
XLA Ops:
  30.6 88.1 %all-to-all-done.5 = bf16[1024,4,512]{2,0,1:T(8,128)(2,1)} async-done(((bf16[1024,4,512]{2,0,1:T(8,128)(2,1)}), bf16[1024,4,512]{2,0,1:T(8,128)(2,1)}, u32[]{:S(2)}, u32[]{:S(2)}) %all-to-all-start.5) | async-done | bytes 4194336 | tf_op jit(solution)/shard_map/all_to_all | solution.py:144
  128.1 88.1 %all-to-all-done.3 = bf16[1024,4,512]{2,0,1:T(8,128)(2,1)} async-done(((bf16[1024,4,512]{2,0,1:T(8,128)(2,1)}), bf16[1024,4,512]{2,0,1:T(8,128)(2,1)}, u32[]{:S(2)}, u32[]{:S(2)}) %all-to-all-start.3) | async-done | bytes 4194336 | tf_op jit(solution)/shard_map/all_to_all | solution.py:143
  225.7 88.1 %all-to-all-done.2 = bf16[1024,4,512]{2,0,1:T(8,128)(2,1)} async-done(((bf16[1024,4,512]{2,0,1:T(8,128)(2,1)}), bf16[1024,4,512]{2,0,1:T(8,128)(2,1)}, u32[]{:S(2)}, u32[]{:S(2)}) %all-to-all-start.2) | async-done | bytes 4194336 | tf_op jit(solution)/shard_map/all_to_all | solution.py:142
  342.0 69.4 %all-to-all-done.1 = bf16[1024,4,512]{2,0,1:T(8,128)(2,1)} async-done(((bf16[1024,4,512]{2,0,1:T(8,128)(2,1)}), bf16[1024,4,512]{2,0,1:T(8,128)(2,1)}, u32[]{:S(2)}, u32[]{:S(2)}) %all-to-all-start.1) | async-done | bytes 4194336 | tf_op jit(solution)/shard_map/all_to_all | solution.py:141
  430.8 11.8 %multiply_convert_fusion.1 = bf16[32,4,128,128]{3,0,2,1:T(8,128)(2,1)S(1)} fusion(f32[32,4,128,128]{3,2,1,0:T(8,128)S(1)} %get-tuple-element.42, s32[32]{0:T(128)S(1)} %get-tuple-element.47, s32[32]{0:T(128)S(1)} %get-tuple-element.46, pred[32]{0:T(512)(128)(4,1)S(1)} %fusion.227), kind=kOutput, calls=%fused_computation.75 | convolution fusion | flops 809503744 | bytes 12583200 | tf_op jit(solution)/shard_map/ij,jgde->igde/dot_general | solution.py:85
  450.5 12.1 %multiply_convert_fusion.2 = bf16[32,4,128,128]{3,0,2,1:T(8,128)(2,1)S(1)} fusion(f32[32,4,128,128]{3,2,1,0:T(8,128)S(1)} %get-tuple-element.42, s32[32]{0:T(128)S(1)} %get-tuple-element.49, s32[32]{0:T(128)S(1)} %get-tuple-element.48, pred[32]{0:T(512)(128)(4,1)S(1)} %fusion.226), kind=kOutput, calls=%fused_computation.76 | convolution fusion | flops 809503744 | bytes 12583200 | tf_op jit(solution)/shard_map/ij,jgde->igde/dot_general | solution.py:85
  464.6 7.9 fusion.77
  472.5 10.5 fusion.75
  483.0 10.7 fusion.79
  493.7 11.8 %multiply_convert_fusion.3 = bf16[32,4,128,128]{3,0,2,1:T(8,128)(2,1)S(1)} fusion(f32[32,4,128,128]{3,2,1,0:T(8,128)S(1)} %get-tuple-element.42, s32[32]{0:T(128)S(1)} %get-tuple-element.51, s32[32]{0:T(128)S(1)} %get-tuple-element.50, pred[32]{0:T(512)(128)(4,1)S(1)} %fusion.225), kind=kOutput, calls=%fused_computation.77 | convolution fusion | flops 809503744 | bytes 12583200 | tf_op jit(solution)/shard_map/ij,jgde->igde/dot_general | solution.py:85
  515.4 10.6 fusion.83
  526.0 11.7 %multiply_convert_fusion.5 = bf16[32,4,128,128]{3,0,2,1:T(8,128)(2,1)S(1)} fusion(f32[32,4,128,128]{3,2,1,0:T(8,128)S(1)} %get-tuple-element.42, s32[32]{0:T(128)S(1)} %broadcast_multiply_fusion.3, pred[32]{0:T(512)(128)(4,1)S(1)} %fusion.223), kind=kOutput, calls=%fused_computation.79 | convolution fusion | flops 809503744 | bytes 12583072 | tf_op jit(solution)/shard_map/ij,jgde->igde/dot_general | solution.py:85
  537.7 7.9 fusion.89
  545.7 15.8 %multiply_convert_fusion.4 = bf16[32,4,128,128]{3,0,2,1:T(8,128)(2,1)S(1)} fusion(f32[32,4,128,128]{3,2,1,0:T(8,128)} %copy-done.9, s32[32]{0:T(128)S(1)} %get-tuple-element.53, s32[32]{0:T(128)S(1)} %get-tuple-element.52, pred[32]{0:T(512)(128)(4,1)S(1)} %fusion.224), kind=kOutput, calls=%fused_computation.78 | convolution fusion | flops 809503744 | bytes 12583200 | tf_op jit(solution)/shard_map/ij,jgde->igde/dot_general | solution.py:85
  561.6 8.0 fusion.85
  576.9 13.1 %fusion.32 = f32[32,4,128,128]{3,0,2,1:T(8,128)} fusion(f32[32,4,128,128]{3,2,1,0:T(8,128)S(1)} %fusion.56, s32[32]{0:T(128)S(1)} %get-tuple-element.47, s32[32]{0:T(128)S(1)} %get-tuple-element.46, pred[32]{0:T(512)(128)(4,1)S(1)} %fusion.227), kind=kOutput, calls=%fused_computation.62 | convolution fusion | flops 805309440 | bytes 16777504 | tf_op jit(solution)/shard_map/ij,igde->jgde/dot_general | solution.py:93
  596.7 11.1 multiply_reduce_fusion
  632.3 25.6 %fusion.13 = (bf16[32,128,4]{1,2,0:T(4,128)(2,1)S(1)}, bf16[32,128,4]{1,2,0:T(4,128)(2,1)}, bf16[32,128,4]{1,2,0:T(4,128)(2,1)S(1)}, bf16[32,128,4]{1,2,0:T(4,12...) fusion(bf16[32,128,4,128]{3,2,1,0:T(4,128)(2,1)S(1)} %copy-done, ...), kind=kOutput, calls=%fused_computation.27 | convolution fusion | flops 568213504 | bytes 67469312 | tf_op jit(solution)/shard_map/ntgd,gde->ntge/dot_general | solution.py:99
  671.6 26.1 %fusion.25 = bf16[32,128,4,128]{3,1,2,0:T(8,128)(2,1)S(1)} fusion(f32[4,128,32,128]{1,3,0,2:T(8,128)} %get-tuple-element.45, f32[4,128,32,128]{1,3,0,2:T(8,128)} %fusion.139, f32[32,4,128,128]{2,3,1,0:T(8,128)} %fusion.73, f32[32,4,128,128]{2,3,1,0:T(8,128)} %fusion.77, f32[32,4,128,128]{2,3,1,0:T(8,128)} %fusion.81, f32[32,4,128,128]{2,3,1,0:T(8,128)} %fusion.85, ...), kind=kOutput, calls=%fused_computation.49 | convolution fusion | flops 574619648 | bytes 76087296 | tf_op jit(solution)/shard_map/ngts,nsgd->ntgd/dot_general | solution.py:43
  716.5 11.9 %fusion.87 = f32[32,4,128,128]{2,3,1,0:T(8,128)} fusion(bf16[32,4,128,128]{3,0,2,1:T(8,128)(2,1)} %copy-done.15, bf16[32,128,4,128]{3,2,1,0:T(4,128)(2,1)} %reshape.630), kind=kOutput, calls=%fused_computation.123 | convolution fusion | flops 536870912 | bytes 16777216 | tf_op jit(solution)/shard_map/ntge,ngde->ntgd/dot_general | solution.py:90
  729.3 17.4 %fusion.34 = f32[32,4,128,128]{3,0,2,1:T(8,128)} fusion(f32[32,4,128,128]{3,2,1,0:T(8,128)} %fusion.58, s32[32]{0:T(128)S(1)} %copy-done.42, s32[32]{0:T(128)S(1)} %copy-done.40, pred[32]{0:T(512)(128)(4,1)S(1)} %copy-done.38), kind=kOutput, calls=%fused_computation.64 | convolution fusion | flops 805309440 | bytes 16777504 | tf_op jit(solution)/shard_map/ij,igde->jgde/dot_general | solution.py:93
  753.4 8.6 fusion.105
  775.4 21.7 %fusion.17 = bf16[32,128,4,128]{3,1,2,0:T(8,128)(2,1)} fusion(f32[4,128,32,128]{1,3,0,2:T(8,128)} %fusion.133, f32[4,128,32,128]{1,3,0,2:T(8,128)} %fusion.137, f32[32,4,128,128]{2,3,1,0:T(8,128)S(1)} %bitcast.276, f32[32,4,128,128]{2,3,1,0:T(8,128)S(1)} %bitcast.278, f32[32,4,128,128]{2,3,1,0:T(8,128)} %fusion.83, f32[32,4,128,128]{2,3,1,0:T(8,128)} %fusion.87, ...), kind=kOutput, calls=%fused_computation.34 | convolution fusion | flops 568328192 | bytes 71761920 | tf_op jit(solution)/shard_map/ntge,ngde->ntgd/dot_general | solution.py:90
  797.0 8.2 copy.351
  817.3 17.2 %fusion.36 = f32[32,4,128,128]{3,0,2,1:T(8,128)} fusion(f32[32,4,128,128]{3,2,1,0:T(8,128)} %fusion.60, s32[32]{0:T(128)S(1)} %copy-done.36, s32[32]{0:T(128)S(1)} %copy-done.34, pred[32]{0:T(512)(128)(4,1)S(1)} %copy-done.28), kind=kOutput, calls=%fused_computation.66 | convolution fusion | flops 805309440 | bytes 16777504 | tf_op jit(solution)/shard_map/ij,igde->jgde/dot_general | solution.py:93
  842.1 13.4 %fusion.38 = f32[32,4,128,128]{3,0,2,1:T(8,128)} fusion(f32[32,4,128,128]{3,2,1,0:T(8,128)S(1)} %fusion.62, s32[32]{0:T(128)S(1)} %copy-done.32, s32[32]{0:T(128)S(1)} %copy-done.30, pred[32]{0:T(512)(128)(4,1)S(1)} %copy-done.26), kind=kOutput, calls=%fused_computation.68 | convolution fusion | flops 805309440 | bytes 16777504 | tf_op jit(solution)/shard_map/ij,igde->jgde/dot_general | solution.py:93
  874.4 25.1 %add_convert_fusion = bf16[32,4,128,128]{3,0,2,1:T(8,128)(2,1)} fusion(f32[32,4,128,128]{3,0,2,1:T(8,128)} %fusion.32, f32[32,4,128,128]{3,0,2,1:T(8,128)} %fusion.34, f32[32,4,128,128]{3,0,2,1:T(8,128)} %fusion.36, f32[32,4,128,128]{3,0,2,1:T(8,128)} %fusion.38, f32[4,128,128]{2,1,0:T(8,128)S(1)} %bitcast.294, f32[4,128,128]{2,1,0:T(8,128)S(1)} %bitcast.293, ...), kind=kOutput, calls=%fused_computation.73 | convolution fusion | flops 830475264 | bytes 46661792 | tf_op jit(solution)/shard_map/ij,igde->jgde/dot_general | solution.py:93
  932.8 9.4 fusion.129
  942.2 9.8 fusion.14
  952.0 8.2 copy.383
  967.3 58.1 %all-to-all-done.7 = bf16[4,1024,512]{2,1,0:T(8,128)(2,1)} async-done(((bf16[4,1024,512]{2,1,0:T(8,128)(2,1)}), bf16[4,1024,512]{2,1,0:T(8,128)(2,1)}, u32[]{:S(2)}, u32[]{:S(2)}) %all-to-all-start.7) | async-done | bytes 4194336 | tf_op jit(solution)/shard_map/all_to_all | solution.py:171
  1069.0 54.0 %all-to-all-done.8 = bf16[4,1024,512]{2,1,0:T(8,128)(2,1)} async-done(((bf16[4,1024,512]{2,1,0:T(8,128)(2,1)}), bf16[4,1024,512]{2,1,0:T(8,128)(2,1)}, u32[]{:S(2)}, u32[]{:S(2)}) %all-to-all-start.8) | async-done | bytes 4194336 | tf_op jit(solution)/shard_map/all_to_all | solution.py:172
  (215 shorter events, 336.4 us)
Async XLA Ops:
  9.0 12.2 %all-to-all-start = ((bf16[1024,4,32]{0,2,1:T(8,128)(2,1)}), bf16[1024,4,32]{0,2,1:T(8,128)(2,1)S(1)}, u32[]{:S(2)}, u32[]{:S(2)}) async-start(bf16[1024,4,32]{0,2,1:T(8,128)(2,1)} %bitcast), calls=%async_computation | async-start | bytes 524288 | tf_op jit(solution)/shard_map/all_to_all | solution.py:145
  21.1 97.5 %all-to-all-start.5 = ((bf16[1024,4,512]{2,0,1:T(8,128)(2,1)}), bf16[1024,4,512]{2,0,1:T(8,128)(2,1)}, u32[]{:S(2)}, u32[]{:S(2)}) async-start(bf16[1024,4,512]{2,0,1:T(8,128)(2,1)} %bitcast.280), calls=%async_computation.5 | async-start | bytes 8388608 | tf_op jit(solution)/shard_map/all_to_all | solution.py:144
  118.7 97.5 %all-to-all-start.3 = ((bf16[1024,4,512]{2,0,1:T(8,128)(2,1)}), bf16[1024,4,512]{2,0,1:T(8,128)(2,1)}, u32[]{:S(2)}, u32[]{:S(2)}) async-start(bf16[1024,4,512]{2,0,1:T(8,128)(2,1)} %bitcast.281), calls=%async_computation.3 | async-start | bytes 8388608 | tf_op jit(solution)/shard_map/all_to_all | solution.py:143
  216.2 97.6 %all-to-all-start.2 = ((bf16[1024,4,512]{2,0,1:T(8,128)(2,1)}), bf16[1024,4,512]{2,0,1:T(8,128)(2,1)}, u32[]{:S(2)}, u32[]{:S(2)}) async-start(bf16[1024,4,512]{2,0,1:T(8,128)(2,1)} %bitcast.282), calls=%async_computation.2 | async-start | bytes 8388608 | tf_op jit(solution)/shard_map/all_to_all | solution.py:142
  313.8 97.6 %all-to-all-start.1 = ((bf16[1024,4,512]{2,0,1:T(8,128)(2,1)}), bf16[1024,4,512]{2,0,1:T(8,128)(2,1)}, u32[]{:S(2)}, u32[]{:S(2)}) async-start(bf16[1024,4,512]{2,0,1:T(8,128)(2,1)} %bitcast.279), calls=%async_computation.1 | async-start | bytes 8388608 | tf_op jit(solution)/shard_map/all_to_all | solution.py:141
  318.7 301.9 %all-gather.5.cloned.1.call-start = ((), (), s32[]{:S(2)}) async-start(), calls=%async_computation.10 | async-start | bytes 1310720 | tf_op jit(solution)/shard_map/all_gather | solution.py:154
  318.9 207.1 %copy-start.43 = (s32[32]{0:T(128)}, s32[32]{0:T(128)S(1)}, u32[]{:S(2)}) copy-start(s32[32]{0:T(128)S(1)} %broadcast_multiply_fusion.3) | copy-start | bytes 388
  318.9 207.1 %copy-start.45 = (pred[32]{0:T(512)(128)(4,1)}, pred[32]{0:T(512)(128)(4,1)S(1)}, u32[]{:S(2)}) copy-start(pred[32]{0:T(512)(128)(4,1)S(1)} %fusion.223) | copy-start | bytes 100
  319.0 131.5 %copy-start.37 = (pred[32]{0:T(512)(128)(4,1)}, pred[32]{0:T(512)(128)(4,1)S(1)}, u32[]{:S(2)}) copy-start(pred[32]{0:T(512)(128)(4,1)S(1)} %fusion.226) | copy-start | bytes 100
  319.0 174.7 %copy-start.27 = (pred[32]{0:T(512)(128)(4,1)}, pred[32]{0:T(512)(128)(4,1)S(1)}, u32[]{:S(2)}) copy-start(pred[32]{0:T(512)(128)(4,1)S(1)} %fusion.225) | copy-start | bytes 100
  319.0 226.7 %copy-start.25 = (pred[32]{0:T(512)(128)(4,1)}, pred[32]{0:T(512)(128)(4,1)S(1)}, u32[]{:S(2)}) copy-start(pred[32]{0:T(512)(128)(4,1)S(1)} %fusion.224) | copy-start | bytes 100
  319.5 131.0 %copy-start.39 = (s32[32]{0:T(128)}, s32[32]{0:T(128)S(1)}, u32[]{:S(2)}) copy-start(s32[32]{0:T(128)S(1)} %get-tuple-element.48) | copy-start | bytes 388
  319.5 131.0 %copy-start.41 = (s32[32]{0:T(128)}, s32[32]{0:T(128)S(1)}, u32[]{:S(2)}) copy-start(s32[32]{0:T(128)S(1)} %get-tuple-element.49) | copy-start | bytes 388
  319.5 174.2 %copy-start.33 = (s32[32]{0:T(128)}, s32[32]{0:T(128)S(1)}, u32[]{:S(2)}) copy-start(s32[32]{0:T(128)S(1)} %get-tuple-element.50) | copy-start | bytes 388
  319.5 174.2 %copy-start.35 = (s32[32]{0:T(128)}, s32[32]{0:T(128)S(1)}, u32[]{:S(2)}) copy-start(s32[32]{0:T(128)S(1)} %get-tuple-element.51) | copy-start | bytes 388
  319.5 226.2 %copy-start.29 = (s32[32]{0:T(128)}, s32[32]{0:T(128)S(1)}, u32[]{:S(2)}) copy-start(s32[32]{0:T(128)S(1)} %get-tuple-element.52) | copy-start | bytes 388
  319.5 226.2 %copy-start.31 = (s32[32]{0:T(128)}, s32[32]{0:T(128)S(1)}, u32[]{:S(2)}) copy-start(s32[32]{0:T(128)S(1)} %get-tuple-element.53) | copy-start | bytes 388
  424.5 101.5 %copy-start.9 = (f32[32,4,128,128]{3,2,1,0:T(8,128)}, f32[32,4,128,128]{3,2,1,0:T(8,128)S(1)}, u32[]{:S(2)}) copy-start(f32[32,4,128,128]{3,2,1,0:T(8,128)S(1)} %get-tuple-element.42) | copy-start | bytes 25165828
  545.7 15.8 %copy-start.6 = (bf16[32,128,4,128]{3,2,1,0:T(4,128)(2,1)S(1)}, bf16[32,128,4,128]{3,2,1,0:T(4,128)(2,1)}, u32[]{:S(2)}) copy-start(bf16[32,128,4,128]{3,2,1,0:T(4,128)(2,1)} %reshape.627) | copy-start | bytes 12582916
  667.8 43.0 %all-to-all-start.9 = ((bf16[4,1024,32]{1,2,0:T(8,128)(2,1)}), bf16[4,1024,32]{1,2,0:T(8,128)(2,1)S(1)}, u32[]{:S(2)}, u32[]{:S(2)}) async-start(bf16[4,1024,32]{1,2,0:T(8,128)(2,1)} %copy.387), calls=%async_computation.9 | async-start | bytes 524288 | tf_op jit(solution)/shard_map/all_to_all | solution.py:173
  711.5 100.9 %all-to-all-start.4 = ((bf16[4,1024,512]{2,1,0:T(8,128)(2,1)}), bf16[4,1024,512]{2,1,0:T(8,128)(2,1)}, u32[]{:S(2)}, u32[]{:S(2)}) async-start(bf16[4,1024,512]{2,1,0:T(8,128)(2,1)} %convert_element_type.131), calls=%async_computation.4 | async-start | bytes 8388608 | tf_op jit(solution)/shard_map/all_to_all | solution.py:169
  716.4 12.9 %copy-start.38 = (pred[32]{0:T(512)(128)(4,1)S(1)}, pred[32]{0:T(512)(128)(4,1)}, u32[]{:S(2)}) copy-start(pred[32]{0:T(512)(128)(4,1)} %copy-done.37) | copy-start | bytes 100
  716.4 150.5 %all-gather.7.cloned.1.call-start = ((), (), s32[]{:S(2)}) async-start(), calls=%async_computation.11 | async-start | bytes 2621440 | tf_op jit(solution)/shard_map/all_gather | solution.py:155
  729.3 17.5 %copy-start.3 = (bf16[32,128,4,128]{3,2,1,0:T(4,128)(2,1)S(1)}, bf16[32,128,4,128]{3,2,1,0:T(4,128)(2,1)}, u32[]{:S(2)}) copy-start(bf16[32,128,4,128]{3,2,1,0:T(4,128)(2,1)} %reshape.630) | copy-start | bytes 12582916
  729.3 17.5 %copy-start.7 = (bf16[32,128,4,128]{3,2,1,0:T(4,128)(2,1)S(1)}, bf16[32,128,4,128]{3,2,1,0:T(4,128)(2,1)}, u32[]{:S(2)}) copy-start(bf16[32,128,4,128]{3,2,1,0:T(4,128)(2,1)} %reshape.627) | copy-start | bytes 12582916
  812.4 115.1 %all-to-all-start.6 = ((bf16[4,1024,512]{2,1,0:T(8,128)(2,1)}), bf16[4,1024,512]{2,1,0:T(8,128)(2,1)}, u32[]{:S(2)}, u32[]{:S(2)}) async-start(bf16[4,1024,512]{2,1,0:T(8,128)(2,1)} %convert_element_type.134), calls=%async_computation.6 | async-start | bytes 8388608 | tf_op jit(solution)/shard_map/all_to_all | solution.py:170
  817.3 17.3 %copy-start.4 = (bf16[32,128,4,128]{3,2,1,0:T(4,128)(2,1)S(1)}, bf16[32,128,4,128]{3,2,1,0:T(4,128)(2,1)}, u32[]{:S(2)}) copy-start(bf16[32,128,4,128]{3,2,1,0:T(4,128)(2,1)} %reshape.630) | copy-start | bytes 12582916
  817.3 17.3 %copy-start.8 = (bf16[32,128,4,128]{3,2,1,0:T(4,128)(2,1)S(1)}, bf16[32,128,4,128]{3,2,1,0:T(4,128)(2,1)}, u32[]{:S(2)}) copy-start(bf16[32,128,4,128]{3,2,1,0:T(4,128)(2,1)} %reshape.627) | copy-start | bytes 12582916
  842.1 20.2 %slice-start = ((s8[8388608]{0:T(1024)(128)(4,1)}), s8[4194304]{0:T(1024)(128)(4,1)S(1)}, s32[]{:S(2)}) async-start(s8[8388608]{0:T(1024)(128)(4,1)} %bitcast.273), calls=%async_computation.12 | async-start | bytes 8388608
  927.5 97.9 %all-to-all-start.7 = ((bf16[4,1024,512]{2,1,0:T(8,128)(2,1)}), bf16[4,1024,512]{2,1,0:T(8,128)(2,1)}, u32[]{:S(2)}, u32[]{:S(2)}) async-start(bf16[4,1024,512]{2,1,0:T(8,128)(2,1)} %convert_element_type.145), calls=%async_computation.7 | async-start | bytes 8388608 | tf_op jit(solution)/shard_map/all_to_all | solution.py:171
  967.3 63.0 %copy-start.21 = (bf16[4,1024,32]{1,2,0:T(8,128)(2,1)S(1)}, bf16[4,1024,32]{1,2,0:T(8,128)(2,1)}, u32[]{:S(2)}) copy-start(bf16[4,1024,32]{1,2,0:T(8,128)(2,1)} %copy-done.20) | copy-start | bytes 786436
  1025.4 97.5 %all-to-all-start.8 = ((bf16[4,1024,512]{2,1,0:T(8,128)(2,1)}), bf16[4,1024,512]{2,1,0:T(8,128)(2,1)}, u32[]{:S(2)}, u32[]{:S(2)}) async-start(bf16[4,1024,512]{2,1,0:T(8,128)(2,1)} %convert_element_type.147), calls=%async_computation.8 | async-start | bytes 8388608 | tf_op jit(solution)/shard_map/all_to_all | solution.py:172
  (33 other events, 243.7 us)
Sparse Core Ops, SparseCore 0:
  545.8 15.8 all-gather.4
  729.4 24.2 all-gather.6
where the time goes:
time: 1150 us; the launch traced here: 1140 us
  waiting for transfers between devices  449 us (39%)
  matrix products  444 us (39%)
  local copies, waits for them, and re-layouts  183 us (16%)
  starting transfers between devices  47.8 us (4%)
  between operations  15.2 us (1%)
    all_to_all x1, waiting for transfers between devices, shards(): lax.all_to_all(grad_out, 'head', split_axis=1, concat_axis=0, tiled=True)  88.1 us
    all_to_all x1, waiting for transfers between devices, shards(): lax.all_to_all(value, 'head', split_axis=1, concat_axis=0, tiled=True)  88.1 us
    all_to_all x1, waiting for transfers between devices, shards(): lax.all_to_all(key, 'head', split_axis=1, concat_axis=0, tiled=True)  88.1 us
    dot_general x5, matrix products, finish(): jnp.einsum('ij,igde->jgde', mapping, products[level - 1], precision=lax.P...  86.3 us
    all_to_all x1, waiting for transfers between devices, shards(): lax.all_to_all(query, 'head', split_axis=1, concat_axis=0, tiled=True)  69.4 us
    dot_general x5, matrix products, finish(): jnp.einsum('ntge,ngde->ntgd', grad_blocks, read_state, preferred_element_...  65.4 us
    dot_general x5, matrix products, finish(): jnp.einsum('ij,jgde->igde', mapping, states, precision=lax.Precision.HIGH...  63.1 us
    all_to_all x1, waiting for transfers between devices, shards(): lax.all_to_all(results[2], 'head', split_axis=0, concat_axis=1, tiled=True)  58.1 us
  transfers between devices with their start and end apart: 12, of which 7 were waited for; matrix products, arithmetic and copies ran while one was open for 38% of the time, Pallas kernels for 0%

commit v1 on v0

v1 whole, which is shorter than its diff:
```python
import functools
import math

import jax
import jax.numpy as jnp
from jax import lax
from jax.experimental import pallas as pl
from jax.experimental.pallas import tpu as pltpu
from jax.sharding import PartitionSpec as P

DH = 128
C = 128
LEVELS = 8
AXES = ("seq", "head")
VMEM_LIMIT = 50 * 2**20
BF = jnp.bfloat16
F32 = jnp.float32


def level_scale(level):
    if level == 0:
        return 1.0 / math.sqrt(DH * C)
    return 1.0 / math.sqrt(DH * C * 2 ** (level - 1))


def nn(a, b):
    return lax.dot_general(a, b, (((1,), (0,)), ((), ())), preferred_element_type=F32)


def nt(a, b):
    return lax.dot_general(a, b, (((1,), (1,)), ((), ())), preferred_element_type=F32)


def tn(a, b):
    return lax.dot_general(a, b, (((0,), (0,)), ((), ())), preferred_element_type=F32)


def cat(parts, axis):
    return parts[0] if len(parts) == 1 else jnp.concatenate(parts, axis=axis)


def head_weights(w_ref, head):
    width = w_ref.shape[1]
    return pltpu.roll(w_ref[...].astype(F32), lax.rem(width - head * LEVELS, width), 1)


def pick(rows, head, level, width):
    lane = lax.broadcasted_iota(jnp.int32, (rows, width), 1)
    return jnp.where(lane == head * LEVELS + level, 1.0, 0.0).astype(BF)


def sums_kernel(local_bits, q_ref, k_ref, v_ref, g_ref, w_ref, t_ref, *rest):
    p_refs, wr = rest[:-1], rest[-1]
    head = pl.program_id(0)
    wr[...] = head_weights(w_ref, head)
    t_ref[0] = tn(k_ref[...], v_ref[...]).astype(BF)
    q = q_ref[...].astype(F32)
    weighted = [
        (wr[:, local_bits + 1 + j : local_bits + 2 + j] * q).astype(BF) for j in range(len(p_refs))
    ]
    out = tn(g_ref[...], cat(weighted, 1))
    for j, p_ref in enumerate(p_refs):
        p_ref[0] = out[:, j * DH : (j + 1) * DH].astype(BF)


def sums_call(query, key, value, grad_out, weights, heads, local_bits, cross_bits):
    tokens = query.shape[0]
    column = pl.BlockSpec((tokens, DH), lambda h: (0, h))
    square = pl.BlockSpec((1, DH, DH), lambda h: (h, 0, 0))
    outs = [jax.ShapeDtypeStruct((heads, DH, DH), BF)] * (1 + cross_bits)
    return pl.pallas_call(
        functools.partial(sums_kernel, local_bits),
        grid=(heads,),
        in_specs=[column] * 4 + [pl.BlockSpec(weights.shape, lambda h: (0, 0))],
        out_specs=[square] * (1 + cross_bits),
        out_shape=outs,
        scratch_shapes=[pltpu.VMEM(weights.shape, F32)],
        compiler_params=pltpu.CompilerParams(vmem_limit_bytes=VMEM_LIMIT),
        name="sums",
    )(query, key, value, grad_out, weights)


def local_kernel(first_head, stretches, aliased, *refs):
    q_ref, k_ref, v_ref, g_ref, w_ref = refs[:5]
    att_ref, dq_ref, dk_ref, dv_ref, gw_ref, wr = refs[5 + aliased :]
    step = pl.program_id(0)
    head = first_head + step
    local_bits = stretches.bit_length() - 1
    width = w_ref.shape[1]

    @pl.when(step == 0)
    def _():
        gw_ref[...] = jnp.zeros_like(gw_ref)

    wr[...] = head_weights(w_ref, head)

    def rows(ref, n, count=1):
        return ref[n * C : (n + count) * C, :]

    def weighted(n, level):
        return (wr[n * C : (n + 1) * C, level : level + 1] * rows(q_ref, n).astype(F32)).astype(BF)

    sums = {}
    for n in range(stretches - 1):
        sums[0, n] = tn(rows(k_ref, n), rows(v_ref, n))
    for b in range(1, local_bits):
        for m in range(stretches >> b):
            if (b - 1, 2 * m + 1) in sums:
                sums[b, m] = sums[b - 1, 2 * m] + sums[b - 1, 2 * m + 1]
    states, adjoints, wq = {}, {}, {}
    for b in range(local_bits):
        for group in range(stretches >> (b + 1)):
            states[b, group] = (level_scale(b + 1) * sums[b, 2 * group]).astype(BF)
            first = (2 * group + 1) << b
            for n in range(first, first + (1 << b)):
                wq[b, n] = weighted(n, b + 1)
            up = cat([wq[b, n] for n in range(first, first + (1 << b))], 0)
            adjoints[b, group] = level_scale(b + 1) * tn(rows(g_ref, first, 1 << b), up)

    row = lax.broadcasted_iota(jnp.int32, (C, C), 0)
    col = lax.broadcasted_iota(jnp.int32, (C, C), 1)
    mask = jnp.where(col <= row, level_scale(0), 0.0).astype(F32)
    for n in range(stretches):
        q, k, v, g = (rows(ref, n) for ref in (q_ref, k_ref, v_ref, g_ref))
        here = slice(n * C, (n + 1) * C)
        bits = [b for b in range(local_bits) if n >> b & 1]
        read = [states[b, n >> (b + 1)] for b in bits]
        scores = nt(q, k) * mask
        grads = nt(g, v)
        w0 = wr[here, 0:1]
        probs = (w0 * scores).astype(BF)
        gscores = (w0 * (grads * mask)).astype(BF)
        att = nn(cat([probs] + [wq[b, n] for b in bits], 1), cat([v] + read, 0))
        dq = nn(gscores, k)
        marks = [(scores * grads).astype(BF)]
        q32 = q.astype(F32)
        for b, state in zip(bits, read):
            back = nt(g, state)
            dq = dq + wr[here, b + 1 : b + 2] * back
            marks.append((q32 * back).astype(BF))
        picks = [pick(C, head, level, width) for level in [0] + [b + 1 for b in bits]]
        gw_ref[here, :] += nn(cat(marks, 1), cat(picks, 0))
        dk = tn(gscores, q)
        dv = tn(probs, g)
        adjoint = None
        for b in range(local_bits):
            if not n >> b & 1:
                term = adjoints[b, n >> (b + 1)]
                adjoint = term if adjoint is None else adjoint + term
        if adjoint is not None:
            adjoint = adjoint.astype(BF)
            dk = dk + nn(v, adjoint)
            dv = dv + nt(k, adjoint)
        att_ref[here, :] = att.astype(BF)
        dq_ref[here, :] = dq.astype(BF)
        dk_ref[here, :] = dk.astype(BF)
        dv_ref[here, :] = dv.astype(BF)


def local_call(query, key, value, grad_out, weights, partial, first_head, count):
    tokens = query.shape[0]
    stretches = tokens // C
    column = pl.BlockSpec((tokens, DH), lambda h: (0, first_head + h))
    whole = pl.BlockSpec(weights.shape, lambda h: (0, 0))
    shape = jax.ShapeDtypeStruct(query.shape, BF)
    flops = 2 * count * stretches * 18 * C * C * C
    return pl.pallas_call(
        functools.partial(local_kernel, first_head, stretches, len(partial)),
        grid=(count,),
        in_specs=[column] * 4 + [whole] + [pl.BlockSpec(memory_space=pl.ANY)] * len(partial),
        out_specs=[column] * 4 + [whole],
        out_shape=[shape] * 4 + [jax.ShapeDtypeStruct(weights.shape, F32)],
        scratch_shapes=[pltpu.VMEM(weights.shape, F32)],
        input_output_aliases={5 + i: i for i in range(len(partial))},
        compiler_params=pltpu.CompilerParams(vmem_limit_bytes=VMEM_LIMIT),
        cost_estimate=pl.CostEstimate(
            flops=flops * 8, bytes_accessed=count * tokens * DH * 16, transcendentals=0
        ),
        name="local",
    )(query, key, value, grad_out, weights, *partial)


def cross_kernel(local_bits, cross_bits, chunks, *refs):
    q_ref, k_ref, v_ref, g_ref, w_ref = refs[:5]
    att_in, dq_in, dk_in, dv_in = refs[5:9]
    gw_in = refs[9 : 9 + chunks]
    states = refs[9 + chunks : 9 + chunks + cross_bits]
    adjoint = refs[9 + chunks + cross_bits]
    att_ref, dq_ref, dk_ref, dv_ref, gw_ref, acc, wr = refs[10 + chunks + cross_bits :]
    head = pl.program_id(0)
    width = w_ref.shape[1]

    @pl.when(head == 0)
    def _():
        total = gw_in[0][...]
        for other in gw_in[1:]:
            total = total + other[...]
        acc[...] = total

    wr[...] = head_weights(w_ref, head)
    read = cat([state[0] for state in states], 0)
    adj = adjoint[0]
    picks = cat([pick(DH, head, local_bits + 1 + j, width) for j in range(cross_bits)], 0)
    tokens = q_ref.shape[0]
    step = min(2 * C, tokens)
    for start in range(0, tokens, step):
        here = slice(start, start + step)
        q32 = q_ref[here, :].astype(F32)
        columns = [
            wr[here, local_bits + 1 + j : local_bits + 2 + j] for j in range(cross_bits)
        ]
        att = att_in[here, :].astype(F32) + nn(cat([(w * q32).astype(BF) for w in columns], 1), read)
        back = nt(g_ref[here, :], read)
        dq = dq_in[here, :].astype(F32)
        marks = []
        for j, w in enumerate(columns):
            part = back[:, j * DH : (j + 1) * DH]
            dq = dq + w * part
            marks.append((q32 * part).astype(BF))
        acc[here, :] += nn(cat(marks, 1), picks)
        att_ref[here, :] = att.astype(BF)
        dq_ref[here, :] = dq.astype(BF)
        dk_ref[here, :] = (dk_in[here, :].astype(F32) + nn(v_ref[here, :], adj)).astype(BF)
        dv_ref[here, :] = (dv_in[here, :].astype(F32) + nt(k_ref[here, :], adj)).astype(BF)

    @pl.when(head == pl.num_programs(0) - 1)
    def _():
        gw_ref[...] = acc[...].astype(BF)


def cross_call(query, key, value, grad_out, weights, partial, gws, states, adjoint, local_bits):
    tokens = query.shape[0]
    heads = query.shape[1] // DH
    cross_bits = len(states)
    column = pl.BlockSpec((tokens, DH), lambda h: (0, h))
    whole = pl.BlockSpec(weights.shape, lambda h: (0, 0))
    square = pl.BlockSpec((1, DH, DH), lambda h: (h, 0, 0))
    return pl.pallas_call(
        functools.partial(cross_kernel, local_bits, cross_bits, len(gws)),
        grid=(heads,),
        in_specs=[column] * 4
        + [whole]
        + [column] * 4
        + [whole] * len(gws)
        + [square] * (cross_bits + 1),
        out_specs=[column] * 4 + [whole],
        out_shape=[jax.ShapeDtypeStruct(query.shape, BF)] * 4
        + [jax.ShapeDtypeStruct(weights.shape, BF)],
        scratch_shapes=[pltpu.VMEM(weights.shape, F32), pltpu.VMEM(weights.shape, F32)],
        input_output_aliases={5 + i: i for i in range(4)},
        compiler_params=pltpu.CompilerParams(vmem_limit_bytes=VMEM_LIMIT),
        name="cross",
    )(query, key, value, grad_out, weights, *partial, *gws, *states, adjoint)


def exchange(total, products, local_bits):
    devices = lax.axis_size(AXES)
    me = lax.axis_index(AXES)
    cross_bits = devices.bit_length() - 1
    products = [product for product in products]
    states = []
    adjoint = None
    for i in range(cross_bits):
        stride = 1 << i
        pairs = [(p, p ^ stride) for p in range(devices)]
        if i == cross_bits - 1:
            pairs = [(p, r) for p, r in pairs if p < r]
        other = lax.ppermute(total.astype(BF), AXES, pairs).astype(F32)
        down = [(p, p ^ stride) for p in range(devices) if p & stride]
        term = level_scale(local_bits + i + 1) * lax.ppermute(
            products[i].astype(BF), AXES, down
        ).astype(F32)
        adjoint = term if adjoint is None else adjoint + term
        for j in range(i + 1, cross_bits):
            upper = [(p, p ^ stride) for p in range(devices) if p >> j & 1]
            products[j] = products[j].astype(F32) + lax.ppermute(
                products[j].astype(BF), AXES, upper
            ).astype(F32)
        reads = me // stride % 2 == 1
        states.append(
            jnp.where(reads, level_scale(local_bits + i + 1) * other, 0.0).astype(BF)
        )
        total = total.astype(F32) + other
    return states, adjoint.astype(BF)


def shards(query, key, value, grad_out, weights):
    tokens = query.shape[0]
    heads = query.shape[1] // DH
    stretches = tokens // C
    local_bits = stretches.bit_length() - 1
    cross_bits = LEVELS - 1 - local_bits
    total, *products = sums_call(
        query, key, value, grad_out, weights, heads, local_bits, cross_bits
    )
    chunks = min(4, heads)
    count = heads // chunks
    partial, gws = [], []
    for c in range(chunks):
        *partial, gw = local_call(
            query, key, value, grad_out, weights, partial, c * count, count
        )
        gws.append(gw)
    states, adjoint = exchange(total, products, local_bits)
    return tuple(
        cross_call(
            query, key, value, grad_out, weights, partial, gws, states, adjoint, local_bits
        )
    )


def solution(mesh):
    spec = P(("rep", "seq", "head"), None)
    return jax.shard_map(
        shards, mesh=mesh, in_specs=(spec,) * 5, out_specs=(spec,) * 5, check_vma=False
    )
```

time: 1150 us -> 233 us (0.20)
  matrix products: 444 us -> 0 us
  waiting for transfers between devices: 449 us -> 59.3 us
  local copies, waits for them, and re-layouts: 183 us -> 2.79 us
  Pallas kernels: 0 us -> 109 us
  other arithmetic: 3.75 us -> 19.8 us
  between operations: 15.2 us -> 1.05 us
    all_to_all x10 -> x0, waiting for transfers between devices: 449 us -> none  [the longest x1 88.1 us: shards(): lax.all_to_all(grad_out, 'head', split_axis=1, concat_axis=0, tiled=True)]
    dot_general x42 -> x0, matrix products: 444 us -> none  [the longest x5 86.3 us: finish(): jnp.einsum('ij,igde->jgde', mapping, products[level - 1], precision=lax.P...]
    pallas_call x0 -> x6, Pallas kernels: none -> 109 us  [the longest x4 59.5 us: local_call(): pl.pallas_call(functools.partial(local_kernel, first_head, stretches, len...]
    convert_element_type x13 -> x0, local copies, waits for them, and re-layouts: 66.1 us -> none  [the longest x10 57.8 us: flatten(): return array.reshape(stretches * C, heads * width).astype(jnp.bfloat16)]
    ppermute x0 -> x14, waiting for transfers between devices: none -> 59.3 us  [the longest x4 51.5 us: exchange(): other = lax.ppermute(total.astype(BF), AXES, pairs).astype(F32)]
    all_to_all x10 -> x0, starting transfers between devices: 47.6 us -> none  [the longest x1 5.19 us: shards(): lax.all_to_all(results[2], 'head', split_axis=0, concat_axis=1, tiled=True)]
    all_to_all x8 -> x0, local copies, waits for them, and re-layouts: 43.3 us -> none  [the longest x1 6.32 us: shards(): lax.all_to_all(results[3], 'head', split_axis=0, concat_axis=1, tiled=True)]
    unnamed x119 -> x16, local copies, waits for them, and re-layouts: 43.7 us -> 2.79 us
  transfers between devices with their start and end apart: 12 -> 14, of which waited for: 7 -> 3; matrix products, arithmetic and copies ran while one was open for 38% -> 7% of each run, Pallas kernels for 0% -> 26%
where the time goes in v1:
time: 233 us; the launch traced here: 231 us
  Pallas kernels  109 us (47%)
  waiting for transfers between devices  59.3 us (25%)
  starting transfers between devices  38.6 us (17%)
  other arithmetic  19.8 us (8%)
  local copies, waits for them, and re-layouts  2.79 us (1%)
    pallas_call x4, Pallas kernels, local_call(): pl.pallas_call(functools.partial(local_kernel, first_head, stretches, len...  59.5 us
    ppermute x4, waiting for transfers between devices, exchange(): other = lax.ppermute(total.astype(BF), AXES, pairs).astype(F32)  51.5 us
    pallas_call x1, Pallas kernels, cross_call(): pl.pallas_call(functools.partial(cross_kernel, local_bits, cross_bits, le...  31.2 us
    ppermute x6, starting transfers between devices, exchange(): lax.ppermute(products[j].astype(BF), AXES, upper).astype(F32)  20.4 us
    pallas_call x1, Pallas kernels, sums_call(): pl.pallas_call(functools.partial(sums_kernel, local_bits), grid=(heads,),...  18.4 us
    ppermute x4, starting transfers between devices, exchange(): lax.ppermute(products[i].astype(BF), AXES, down).astype(F32)  10.3 us
    ppermute x4, starting transfers between devices, exchange(): other = lax.ppermute(total.astype(BF), AXES, pairs).astype(F32)  7.85 us
    ppermute x6, waiting for transfers between devices, exchange(): lax.ppermute(products[j].astype(BF), AXES, upper).astype(F32)  7.82 us
  transfers between devices with their start and end apart: 14, of which 3 were waited for; matrix products, arithmetic and copies ran while one was open for 7% of the time, Pallas kernels for 26%

profile of v1, /device:TPU:3, one launch (start us, length us, event | category | flops | bytes accessed | tf_op | source)
XLA Modules:
  0.0 230.7 jit_solution(16317634359144748557)
XLA Ops:
  1.6 18.4 %sums.1 = (bf16[16,128,128]{2,1,0:T(8,128)(2,1)S(1)}, bf16[16,128,128]{2,1,0:T(8,128)(2,1)}, bf16[16,128,128]{2,1,0:T(8,128)(2,1)}, bf16[16,128,128]{2,1,0:T(8,128)(2,1)S(1)}, bf16[16,128,128]{2,1,0:T(8,128)(2,1)S(1)}) custom-call(bf16[1024,2048]{1,0:T(8,128)(2,1)} %refs_0_.9, bf16[1024,2048]{1,0:T(8,128)(2,1)} %refs_1_.9, bf16[1024,2048]{1,0:T(8,128)(2,1)} %refs_2_.9, ...), custom_call_target="tpu_custom_call" | custom-call | tf_op jit(solution)/shard_map/sums/pallas_call | solution.py:71
  20.0 1.3 collective-permute-start.4
  21.3 1.5 collective-permute-start.5
  22.8 4.8 %collective-permute-start.7 = (bf16[16,128,128]{2,1,0:T(8,128)(2,1)S(1)}, bf16[16,128,128]{2,1,0:T(8,128)(2,1)}, u32[]{:S(2)}, u32[]{:S(2)}) collective-permute-start(bf16[16,128,128]{2,1,0:T(8,128)(2,1)S(1)} %get-tuple-element.53), channel_id=1, source_target_pairs={{4,5},{5,4},{6,7},{7,6},{12,13},{13,12},{14,15},{15,14},{20,21},{2... | collective-permute-start | bytes 1572872 | tf_op jit(solution)/shard_map/ppermute | solution.py:276
  27.6 3.3 %collective-permute-start.10 = (bf16[16,128,128]{2,1,0:T(8,128)(2,1)S(1)}, bf16[16,128,128]{2,1,0:T(8,128)(2,1)}, u32[]{:S(2)}, u32[]{:S(2)}) collective-permute-start(bf16[16,128,128]{2,1,0:T(8,128)(2,1)S(1)} %get-tuple-element.54), channel_id=1, source_target_pairs={{8,9},{9,8},{10,11},{11,10},{12,13},{13,12},{14,15},{15,14},{24,25... | collective-permute-start | bytes 1572872 | tf_op jit(solution)/shard_map/ppermute | solution.py:276
  31.0 14.8 %local.4 = (bf16[1024,2048]{1,0:T(8,128)(2,1)}, bf16[1024,2048]{1,0:T(8,128)(2,1)}, bf16[1024,2048]{1,0:T(8,128)(2,1)}, bf16[1024,2048]{1,0:T(8,128)(2,1)}, f32[1024,128]{1,0:T(8,128)S(1)}) custom-call(bf16[1024,2048]{1,0:T(8,128)(2,1)} %refs_0_.9, bf16[1024,2048]{1,0:T(8,128)(2,1)} %refs_1_.9, bf16[1024,2048]{1,0:T(8,128)(2,1)} %refs_2_.9, ...), custom_call_target="tpu_custom_call" | custom-call | flops 19327352832 | bytes 8388608 | tf_op jit(solution)/shard_map/local/pallas_call | solution.py:167
  45.8 14.8 %local.5 = (bf16[1024,2048]{1,0:T(8,128)(2,1)}, bf16[1024,2048]{1,0:T(8,128)(2,1)}, bf16[1024,2048]{1,0:T(8,128)(2,1)}, bf16[1024,2048]{1,0:T(8,128)(2,1)}, f32[1024,128]{1,0:T(8,128)S(1)}) custom-call(bf16[1024,2048]{1,0:T(8,128)(2,1)} %refs_0_.9, ...), custom_call_target="tpu_custom_call", output_to_operand_aliasing={{0}: (5, {}), {1}: (6, {}), {2}: (7, {}), {3}: (8, {})} | custom-call | flops 19327352832 | bytes 8388608 | tf_op jit(solution)/shard_map/local/pallas_call | solution.py:167
  60.6 15.0 %local.6 = (bf16[1024,2048]{1,0:T(8,128)(2,1)}, bf16[1024,2048]{1,0:T(8,128)(2,1)}, bf16[1024,2048]{1,0:T(8,128)(2,1)}, bf16[1024,2048]{1,0:T(8,128)(2,1)}, f32[1024,128]{1,0:T(8,128)S(1)}) custom-call(bf16[1024,2048]{1,0:T(8,128)(2,1)} %refs_0_.9, ...), custom_call_target="tpu_custom_call", output_to_operand_aliasing={{0}: (5, {}), {1}: (6, {}), {2}: (7, {}), {3}: (8, {})} | custom-call | flops 19327352832 | bytes 8388608 | tf_op jit(solution)/shard_map/local/pallas_call | solution.py:167
  75.7 2.3 add_convert_fusion.3
  78.0 1.3 collective-permute-start.6
  79.3 1.2 fusion.9
  80.5 3.8 %collective-permute-start.1 = (bf16[16,128,128]{2,1,0:T(8,128)(2,1)S(1)}, bf16[16,128,128]{2,1,0:T(8,128)(2,1)S(1)}, u32[]{:S(2)}, u32[]{:S(2)}) collective-permute-start(bf16[16,128,128]{2,1,0:T(8,128)(2,1)S(1)} %fusion.9), channel_id=1, source_target_pairs={{0,2},{1,3},{2,0},{3,1},{4,6},{5,7},{6,4},{7,5},{8,10},{9,11},{10,... | collective-permute-start | bytes 1572872 | tf_op jit(solution)/shard_map/ppermute | solution.py:268
  84.3 1.2 fusion.8
  85.5 1.9 collective-permute-start.11
  87.4 1.2 fusion.7
  88.6 4.3 %collective-permute-start.8 = (bf16[16,128,128]{2,1,0:T(8,128)(2,1)S(1)}, bf16[16,128,128]{2,1,0:T(8,128)(2,1)S(1)}, u32[]{:S(2)}, u32[]{:S(2)}) collective-permute-start(bf16[16,128,128]{2,1,0:T(8,128)(2,1)S(1)} %fusion.7), channel_id=1, source_target_pairs={{4,6},{5,7},{6,4},{7,5},{12,14},{13,15},{14,12},{15,13},{20,22},{2... | collective-permute-start | bytes 1572872 | tf_op jit(solution)/shard_map/ppermute | solution.py:276
  92.9 51.5 %collective-permute-done.1 = bf16[16,128,128]{2,1,0:T(8,128)(2,1)S(1)} collective-permute-done((bf16[16,128,128]{2,1,0:T(8,128)(2,1)S(1)}, bf16[16,128,128]{2,1,0:T(8,128)(2,1)S(1)}, u32[]{:S(2)}, u32[]{:S(2)}) %collective-permute-start.1) | collective-permute-done | bytes 524320 | tf_op jit(solution)/shard_map/ppermute | solution.py:268
  144.4 1.3 fusion.11
  145.6 2.7 %collective-permute-start.2 = (bf16[16,128,128]{2,1,0:T(8,128)(2,1)S(1)}, bf16[16,128,128]{2,1,0:T(8,128)(2,1)S(1)}, u32[]{:S(2)}, u32[]{:S(2)}) collective-permute-start(bf16[16,128,128]{2,1,0:T(8,128)(2,1)S(1)} %fusion.11), channel_id=1, source_target_pairs={{0,4},{1,5},{2,6},{3,7},{4,0},{5,1},{6,2},{7,3},{8,12},{9,13},{10,... | collective-permute-start | bytes 1572872 | tf_op jit(solution)/shard_map/ppermute | solution.py:268
  148.3 7.3 %collective-permute-done.11 = bf16[16,128,128]{2,1,0:T(8,128)(2,1)S(1)} collective-permute-done((bf16[16,128,128]{2,1,0:T(8,128)(2,1)S(1)}, bf16[16,128,128]{2,1,0:T(8,128)(2,1)S(1)}, u32[]{:S(2)}, u32[]{:S(2)}) %collective-permute-start.11) | collective-permute-done | bytes 524320 | tf_op jit(solution)/shard_map/ppermute | solution.py:276
  155.6 1.3 fusion.10
  156.9 4.6 %collective-permute-start.12 = (bf16[16,128,128]{2,1,0:T(8,128)(2,1)S(1)}, bf16[16,128,128]{2,1,0:T(8,128)(2,1)S(1)}, u32[]{:S(2)}, u32[]{:S(2)}) collective-permute-start(bf16[16,128,128]{2,1,0:T(8,128)(2,1)S(1)} %fusion.10), channel_id=1, source_target_pairs={{8,12},{9,13},{10,14},{11,15},{12,8},{13,9},{14,10},{15,11},{24,28... | collective-permute-start | bytes 1572872 | tf_op jit(solution)/shard_map/ppermute | solution.py:276
  162.0 2.1 add_convert_fusion.2
  164.1 2.2 collective-permute-start.9
  166.3 2.5 %fusion.6 = (bf16[16,128,128]{2,1,0:T(8,128)(2,1)}, bf16[16,128,128]{2,1,0:T(8,128)(2,1)S(1)}, bf16[16,128,128]{2,1,0:T(8,128)(2,1)S(1)}, bf16[16,128,128]{2,1,0:T(8,128)(2,1)S(1)}) fusion(bf16[16,128,128]{2,1,0:T(8,128)(2,1)S(1)} %collective-permute-done.2, bf16[16,128,128]{2,1,0:T(8,128)(2,1)S(1)} %collective-permute-done.1, ...), kind=kLoop, calls=%fused_computation.12 | loop fusion | flops 4456448 | bytes 4194307 | tf_op jit(solution)/shard_map/convert_element_type | solution.py:268
  168.8 1.3 collective-permute-start.3
  170.1 2.2 add_convert_fusion.1
  172.3 5.6 %collective-permute-start.13 = (bf16[16,128,128]{2,1,0:T(8,128)(2,1)}, bf16[16,128,128]{2,1,0:T(8,128)(2,1)}, u32[]{:S(2)}, u32[]{:S(2)}) collective-permute-start(bf16[16,128,128]{2,1,0:T(8,128)(2,1)} %add_convert_fusion.1), channel_id=1, source_target_pairs={{8,0},{9,1},{10,2},{11,3},{12,4},{13,5},{14,6},{15,7},{24,16},{25,... | collective-permute-start | bytes 1572872 | tf_op jit(solution)/shard_map/ppermute | solution.py:270
  177.8 14.9 %local.7 = (bf16[1024,2048]{1,0:T(8,128)(2,1)}, bf16[1024,2048]{1,0:T(8,128)(2,1)}, bf16[1024,2048]{1,0:T(8,128)(2,1)}, bf16[1024,2048]{1,0:T(8,128)(2,1)}, f32[1024,128]{1,0:T(8,128)S(1)}) custom-call(bf16[1024,2048]{1,0:T(8,128)(2,1)} %refs_0_.9, ...), custom_call_target="tpu_custom_call", output_to_operand_aliasing={{0}: (5, {}), {1}: (6, {}), {2}: (7, {}), {3}: (8, {})} | custom-call | flops 19327352832 | bytes 8388608 | tf_op jit(solution)/shard_map/local/pallas_call | solution.py:167
  193.5 2.0 select_convert_fusion.refs_16_
  195.6 2.7 %add_convert_fusion.refs_17_ = bf16[16,128,128]{2,1,0:T(8,128)(2,1)} fusion(bf16[16,128,128]{2,1,0:T(8,128)(2,1)} %collective-permute-done.13, bf16[16,128,128]{2,1,0:T(8,128)(2,1)} %collective-permute-done.9, bf16[16,128,128]{2,1,0:T(8,128)(2,1)} %collective-permute-done.6, bf16[16,128,128]{2,1,0:T(8,128)(2,1)} %collective-permute-done.4), kind=kLoop, calls=%fused_computation.13 | loop fusion | flops 3145728 | bytes 2621440 | tf_op jit(solution)/shard_map/convert_element_type | solution.py:284
  199.4 31.2 %cross.1 = (bf16[1024,2048]{1,0:T(8,128)(2,1)}, bf16[1024,2048]{1,0:T(8,128)(2,1)}, bf16[1024,2048]{1,0:T(8,128)(2,1)}, bf16[1024,2048]{1,0:T(8,128)(2,1)}, bf16[1024,128]{1,0:T(8,128)(2,1)}) custom-call(bf16[1024,2048]{1,0:T(8,128)(2,1)} %refs_0_.9, ...), custom_call_target="tpu_custom_call", output_to_operand_aliasing={{0}: (5, {}), {1}: (6, {}), {2}: (7, {}), {3}: (8, {})} | custom-call | tf_op jit(solution)/shard_map/cross/pallas_call | solution.py:238
  (29 shorter events, 3.4 us)
Async XLA Ops:
  0.6 1.0 copy-start
  20.0 175.5 %collective-permute-start.4 = (bf16[16,128,128]{2,1,0:T(8,128)(2,1)}, bf16[16,128,128]{2,1,0:T(8,128)(2,1)}, u32[]{:S(2)}, u32[]{:S(2)}) collective-permute-start(bf16[16,128,128]{2,1,0:T(8,128)(2,1)} %get-tuple-element.51), channel_id=1, source_target_pairs={{1,0},{3,2},{5,4},{7,6},{9,8},{11,10},{13,12},{15,14},{17,16},{19,... | collective-permute-start | bytes 1572872 | tf_op jit(solution)/shard_map/ppermute | solution.py:270
  21.3 54.4 %collective-permute-start.5 = (bf16[16,128,128]{2,1,0:T(8,128)(2,1)}, bf16[16,128,128]{2,1,0:T(8,128)(2,1)}, u32[]{:S(2)}, u32[]{:S(2)}) collective-permute-start(bf16[16,128,128]{2,1,0:T(8,128)(2,1)} %get-tuple-element.52), channel_id=1, source_target_pairs={{2,3},{3,2},{6,7},{7,6},{10,11},{11,10},{14,15},{15,14},{18,19},{1... | collective-permute-start | bytes 1572872 | tf_op jit(solution)/shard_map/ppermute | solution.py:276
  22.8 64.7 %collective-permute-start.7 = (bf16[16,128,128]{2,1,0:T(8,128)(2,1)S(1)}, bf16[16,128,128]{2,1,0:T(8,128)(2,1)}, u32[]{:S(2)}, u32[]{:S(2)}) collective-permute-start(bf16[16,128,128]{2,1,0:T(8,128)(2,1)S(1)} %get-tuple-element.53), channel_id=1, source_target_pairs={{4,5},{5,4},{6,7},{7,6},{12,13},{13,12},{14,15},{15,14},{20,21},{2... | collective-permute-start | bytes 1572872 | tf_op jit(solution)/shard_map/ppermute | solution.py:276
  27.6 51.7 %collective-permute-start = (bf16[16,128,128]{2,1,0:T(8,128)(2,1)S(1)}, bf16[16,128,128]{2,1,0:T(8,128)(2,1)}, u32[]{:S(2)}, u32[]{:S(2)}) collective-permute-start(bf16[16,128,128]{2,1,0:T(8,128)(2,1)S(1)} %get-tuple-element.50), channel_id=1, source_target_pairs={{0,1},{1,0},{2,3},{3,2},{4,5},{5,4},{6,7},{7,6},{8,9},{9,8},{10,11... | collective-permute-start | bytes 1572872 | tf_op jit(solution)/shard_map/ppermute | solution.py:268
  27.6 56.7 %collective-permute-start.10 = (bf16[16,128,128]{2,1,0:T(8,128)(2,1)S(1)}, bf16[16,128,128]{2,1,0:T(8,128)(2,1)}, u32[]{:S(2)}, u32[]{:S(2)}) collective-permute-start(bf16[16,128,128]{2,1,0:T(8,128)(2,1)S(1)} %get-tuple-element.54), channel_id=1, source_target_pairs={{8,9},{9,8},{10,11},{11,10},{12,13},{13,12},{14,15},{15,14},{24,25... | collective-permute-start | bytes 1572872 | tf_op jit(solution)/shard_map/ppermute | solution.py:276
  60.6 15.0 %copy-start.2 = (f32[1024,128]{1,0:T(8,128)}, f32[1024,128]{1,0:T(8,128)S(1)}, u32[]{:S(2)}) copy-start(f32[1024,128]{1,0:T(8,128)S(1)} %get-tuple-element.47.refs_10_) | copy-start | bytes 1572868
  75.6 70.0 %copy-start.4 = (f32[1024,128]{1,0:T(8,128)}, f32[1024,128]{1,0:T(8,128)S(1)}, u32[]{:S(2)}) copy-start(f32[1024,128]{1,0:T(8,128)S(1)} %get-tuple-element.48.refs_11_) | copy-start | bytes 1572868
  78.0 117.6 %collective-permute-start.6 = (bf16[16,128,128]{2,1,0:T(8,128)(2,1)}, bf16[16,128,128]{2,1,0:T(8,128)(2,1)}, u32[]{:S(2)}, u32[]{:S(2)}) collective-permute-start(bf16[16,128,128]{2,1,0:T(8,128)(2,1)} %add_convert_fusion.3), channel_id=1, source_target_pairs={{2,0},{3,1},{6,4},{7,5},{10,8},{11,9},{14,12},{15,13},{18,16},{19,... | collective-permute-start | bytes 1572872 | tf_op jit(solution)/shard_map/ppermute | solution.py:270
  80.5 63.9 %collective-permute-start.1 = (bf16[16,128,128]{2,1,0:T(8,128)(2,1)S(1)}, bf16[16,128,128]{2,1,0:T(8,128)(2,1)S(1)}, u32[]{:S(2)}, u32[]{:S(2)}) collective-permute-start(bf16[16,128,128]{2,1,0:T(8,128)(2,1)S(1)} %fusion.9), channel_id=1, source_target_pairs={{0,2},{1,3},{2,0},{3,1},{4,6},{5,7},{6,4},{7,5},{8,10},{9,11},{10,... | collective-permute-start | bytes 1572872 | tf_op jit(solution)/shard_map/ppermute | solution.py:268
  85.5 70.1 %collective-permute-start.11 = (bf16[16,128,128]{2,1,0:T(8,128)(2,1)S(1)}, bf16[16,128,128]{2,1,0:T(8,128)(2,1)S(1)}, u32[]{:S(2)}, u32[]{:S(2)}) collective-permute-start(bf16[16,128,128]{2,1,0:T(8,128)(2,1)S(1)} %fusion.8), channel_id=1, source_target_pairs={{8,10},{9,11},{10,8},{11,9},{12,14},{13,15},{14,12},{15,13},{24,26... | collective-permute-start | bytes 1572872 | tf_op jit(solution)/shard_map/ppermute | solution.py:276
  88.6 73.4 %collective-permute-start.8 = (bf16[16,128,128]{2,1,0:T(8,128)(2,1)S(1)}, bf16[16,128,128]{2,1,0:T(8,128)(2,1)S(1)}, u32[]{:S(2)}, u32[]{:S(2)}) collective-permute-start(bf16[16,128,128]{2,1,0:T(8,128)(2,1)S(1)} %fusion.7), channel_id=1, source_target_pairs={{4,6},{5,7},{6,4},{7,5},{12,14},{13,15},{14,12},{15,13},{20,22},{2... | collective-permute-start | bytes 1572872 | tf_op jit(solution)/shard_map/ppermute | solution.py:276
  145.6 20.7 %collective-permute-start.2 = (bf16[16,128,128]{2,1,0:T(8,128)(2,1)S(1)}, bf16[16,128,128]{2,1,0:T(8,128)(2,1)S(1)}, u32[]{:S(2)}, u32[]{:S(2)}) collective-permute-start(bf16[16,128,128]{2,1,0:T(8,128)(2,1)S(1)} %fusion.11), channel_id=1, source_target_pairs={{0,4},{1,5},{2,6},{3,7},{4,0},{5,1},{6,2},{7,3},{8,12},{9,13},{10,... | collective-permute-start | bytes 1572872 | tf_op jit(solution)/shard_map/ppermute | solution.py:268
  156.9 21.0 %copy-start.1 = (bf16[1024,128]{1,0:T(8,128)(2,1)S(1)}, bf16[1024,128]{1,0:T(8,128)(2,1)}, u32[]{:S(2)}) copy-start(bf16[1024,128]{1,0:T(8,128)(2,1)} %refs_4_.9) | copy-start | bytes 786436
  156.9 13.2 %collective-permute-start.12 = (bf16[16,128,128]{2,1,0:T(8,128)(2,1)S(1)}, bf16[16,128,128]{2,1,0:T(8,128)(2,1)S(1)}, u32[]{:S(2)}, u32[]{:S(2)}) collective-permute-start(bf16[16,128,128]{2,1,0:T(8,128)(2,1)S(1)} %fusion.10), channel_id=1, source_target_pairs={{8,12},{9,13},{10,14},{11,15},{12,8},{13,9},{14,10},{15,11},{24,28... | collective-permute-start | bytes 1572872 | tf_op jit(solution)/shard_map/ppermute | solution.py:276
  164.1 31.5 %collective-permute-start.9 = (bf16[16,128,128]{2,1,0:T(8,128)(2,1)}, bf16[16,128,128]{2,1,0:T(8,128)(2,1)}, u32[]{:S(2)}, u32[]{:S(2)}) collective-permute-start(bf16[16,128,128]{2,1,0:T(8,128)(2,1)} %add_convert_fusion.2), channel_id=1, source_target_pairs={{4,0},{5,1},{6,2},{7,3},{12,8},{13,9},{14,10},{15,11},{20,16},{21,... | collective-permute-start | bytes 1572872 | tf_op jit(solution)/shard_map/ppermute | solution.py:270
  168.8 24.7 %collective-permute-start.3 = (bf16[16,128,128]{2,1,0:T(8,128)(2,1)}, bf16[16,128,128]{2,1,0:T(8,128)(2,1)}, u32[]{:S(2)}, u32[]{:S(2)}) collective-permute-start(bf16[16,128,128]{2,1,0:T(8,128)(2,1)} %get-tuple-element.55), channel_id=1, source_target_pairs={{0,8},{1,9},{2,10},{3,11},{4,12},{5,13},{6,14},{7,15},{16,24},{17,... | collective-permute-start | bytes 1572872 | tf_op jit(solution)/shard_map/ppermute | solution.py:268
  172.3 23.3 %collective-permute-start.13 = (bf16[16,128,128]{2,1,0:T(8,128)(2,1)}, bf16[16,128,128]{2,1,0:T(8,128)(2,1)}, u32[]{:S(2)}, u32[]{:S(2)}) collective-permute-start(bf16[16,128,128]{2,1,0:T(8,128)(2,1)} %add_convert_fusion.1), channel_id=1, source_target_pairs={{8,0},{9,1},{10,2},{11,3},{12,4},{13,5},{14,6},{15,7},{24,16},{25,... | collective-permute-start | bytes 1572872 | tf_op jit(solution)/shard_map/ppermute | solution.py:270
  177.8 20.5 %copy-start.3 = (f32[1024,128]{1,0:T(8,128)S(1)}, f32[1024,128]{1,0:T(8,128)}, u32[]{:S(2)}) copy-start(f32[1024,128]{1,0:T(8,128)} %copy-done.2) | copy-start | bytes 1572868
  177.8 20.5 %copy-start.5 = (f32[1024,128]{1,0:T(8,128)S(1)}, f32[1024,128]{1,0:T(8,128)}, u32[]{:S(2)}) copy-start(f32[1024,128]{1,0:T(8,128)} %copy-done.4) | copy-start | bytes 1572868
  192.8 0.8 copy-start.6
  198.3 1.0 copy-start.7

commit v2 on v1

--- a/solution.py
+++ b/solution.py
@@ -11,8 +11,7 @@
 DH = 128
 C = 128
 LEVELS = 8
-AXES = ("seq", "head")
-VMEM_LIMIT = 50 * 2**20
+VMEM_LIMIT = 60 * 2**20
 BF = jnp.bfloat16
 F32 = jnp.float32
 
@@ -80,11 +79,168 @@
     )(query, key, value, grad_out, weights)
 
 
-def local_kernel(first_head, stretches, aliased, *refs):
+class Exchange:
+    def __init__(self, local_bits, cross_bits, head_bits, heads, chunks):
+        self.local_bits, self.cross_bits, self.head_bits = local_bits, cross_bits, head_bits
+        self.chunks, self.count = chunks, heads // chunks
+        self.heads = heads
+        self.received = cross_bits + cross_bits * (cross_bits + 1) // 2
+        self.sent = cross_bits - 1 + cross_bits * (cross_bits - 1) // 2
+        span = heads - chunks - 3
+        last = max(cross_bits - 1, 1)
+        self.offsets = [heads - chunks - (cross_bits - 1 - i) * span // last for i in range(cross_bits)]
+
+    def scratch(self):
+        sems = pltpu.SemaphoreType.DMA((self.received, self.chunks))
+        return [
+            pltpu.VMEM((self.received, self.heads, DH, DH), BF),
+            pltpu.VMEM((max(self.sent, 1), self.heads, DH, DH), BF),
+            pltpu.VMEM((self.heads, DH, DH), F32),
+            sems,
+            sems,
+        ]
+
+    def bind(self, sources, states, adjoint, scratch):
+        self.sources, self.states, self.adjoint = sources, states, adjoint
+        self.landing, self.sending, self.total, self.send_sem, self.recv_sem = scratch
+        head, seq = lax.axis_index("head"), lax.axis_index("seq")
+        self.bits, self.partners = [], []
+        for i in range(self.cross_bits):
+            name, position, stride = "head", head, 1 << i
+            if i >= self.head_bits:
+                name, position, stride = "seq", seq, 1 << (i - self.head_bits)
+            bit = (position // stride) % 2
+            self.bits.append(bit)
+            self.partners.append({name: position + (1 - 2 * bit) * stride})
+
+    def slot(self, item, i):
+        return i if item == 0 else self.cross_bits + (item - 1) * item // 2 + i
+
+    def source(self, item, i):
+        if i == 0:
+            return self.sources[item]
+        j = item - 1
+        return self.sending.at[i - 1 if item == 0 else self.cross_bits - 1 + j * (j - 1) // 2 + i - 1]
+
+    def items(self, i):
+        last = i == self.cross_bits - 1
+        set_here, clear_here = self.bits[i] == 1, self.bits[i] == 0
+        yield (0, clear_here, set_here) if last else (0, None, None)
+        yield i + 1, set_here, clear_here
+        for j in range(i + 1, self.cross_bits):
+            yield j + 1, self.bits[j] == 1, self.bits[j] == 1
+
+    def copy(self, item, i, chunk):
+        part = pl.ds(chunk * self.count, self.count)
+        slot = self.slot(item, i)
+        return pltpu.make_async_remote_copy(
+            src_ref=self.source(item, i).at[part],
+            dst_ref=self.landing.at[slot, part],
+            send_sem=self.send_sem.at[slot, chunk],
+            recv_sem=self.recv_sem.at[slot, chunk],
+            device_id=self.partners[i],
+            device_id_type=pl.DeviceIdType.MESH,
+        )
+
+    def when(self, condition, body):
+        if condition is None:
+            body()
+        else:
+            pl.when(condition)(body)
+
+    def start(self, i, chunk):
+        for item, sends, _ in self.items(i):
+            self.when(sends, lambda item=item: self.copy(item, i, chunk).start())
+
+    def greet(self):
+        barrier = pltpu.get_barrier_semaphore()
+        for partner in self.partners:
+            pl.semaphore_signal(
+                barrier, inc=1, device_id=partner, device_id_type=pl.DeviceIdType.MESH
+            )
+        pl.semaphore_wait(barrier, self.cross_bits)
+
+        def body(chunk, carry):
+            self.start(0, chunk)
+            return carry
+
+        lax.fori_loop(0, self.chunks, body, 0)
+
+    def arrive(self, i, chunk):
+        part = pl.ds(chunk * self.count, self.count)
+        shape = (self.count, DH, DH)
+        factor = level_scale(self.local_bits + i + 1)
+        last = i == self.cross_bits - 1
+
+        def landed(item):
+            return self.landing[self.slot(item, i), part].astype(F32)
+
+        def add(item):
+            self.source(item, i + 1)[part] = (
+                self.source(item, i)[part].astype(F32) + landed(item)
+            ).astype(BF)
+
+        for item, _, receives in self.items(i):
+            self.when(receives, lambda item=item: self.copy(item, i, chunk).wait_recv())
+            if item == 0:
+                if not last:
+                    add(0)
+            elif item == i + 1:
+                continue
+            else:
+                self.when(receives, lambda item=item: add(item))
+        if not last:
+            self.start(i + 1, chunk)
+
+        @pl.when(self.bits[i] == 1)
+        def _():
+            self.states[i][part] = (factor * landed(0)).astype(BF)
+            if i == 0:
+                self.total[part] = jnp.zeros(shape, F32)
+
+        @pl.when(self.bits[i] == 0)
+        def _():
+            self.states[i][part] = jnp.zeros(shape, BF)
+            if i == 0:
+                self.total[part] = factor * landed(i + 1)
+            else:
+                self.total[part] += factor * landed(i + 1)
+
+        if last:
+            self.adjoint[part] = self.total[part].astype(BF)
+
+    def advance(self, step):
+        pl.when(step == 0)(self.greet)
+        for i in reversed(range(self.cross_bits)):
+            chunk = step - self.offsets[i]
+
+            @pl.when((chunk >= 0) & (chunk < self.chunks))
+            def _(i=i, chunk=chunk):
+                self.arrive(i, chunk)
+
+    def finish(self):
+        def body(chunk, carry):
+            for i in range(self.cross_bits):
+                for item, sends, _ in self.items(i):
+                    self.when(
+                        sends, lambda item=item, i=i: self.copy(item, i, chunk).wait_send()
+                    )
+            return carry
+
+        lax.fori_loop(0, self.chunks, body, 0)
+
+
+def local_kernel(stretches, exchange, *refs):
+    cross_bits = exchange.cross_bits
     q_ref, k_ref, v_ref, g_ref, w_ref = refs[:5]
-    att_ref, dq_ref, dk_ref, dv_ref, gw_ref, wr = refs[5 + aliased :]
+    sources = refs[5 : 6 + cross_bits]
+    outs = refs[6 + cross_bits :]
+    att_ref, dq_ref, dk_ref, dv_ref, gw_ref = outs[:5]
+    states_out = outs[5 : 5 + cross_bits]
+    adjoint_out, wr = outs[5 + cross_bits : 7 + cross_bits]
+    exchange.bind(sources, states_out, adjoint_out, outs[7 + cross_bits :])
     step = pl.program_id(0)
-    head = first_head + step
+    head = step
     local_bits = stretches.bit_length() - 1
     width = w_ref.shape[1]
 
@@ -92,6 +248,7 @@
     def _():
         gw_ref[...] = jnp.zeros_like(gw_ref)
 
+    exchange.advance(step)
     wr[...] = head_weights(w_ref, head)
 
     def rows(ref, n, count=1):
@@ -156,28 +313,36 @@
         dk_ref[here, :] = dk.astype(BF)
         dv_ref[here, :] = dv.astype(BF)
 
-
-def local_call(query, key, value, grad_out, weights, partial, first_head, count):
+    @pl.when(step == pl.num_programs(0) - 1)
+    def _():
+        exchange.finish()
+
+
+def local_call(query, key, value, grad_out, weights, sums, head_bits):
     tokens = query.shape[0]
     stretches = tokens // C
-    column = pl.BlockSpec((tokens, DH), lambda h: (0, first_head + h))
+    heads = query.shape[1] // DH
+    cross_bits = len(sums) - 1
+    exchange = Exchange(stretches.bit_length() - 1, cross_bits, head_bits, heads, 4)
+    column = pl.BlockSpec((tokens, DH), lambda h: (0, h))
     whole = pl.BlockSpec(weights.shape, lambda h: (0, 0))
+    squares = pl.BlockSpec((heads, DH, DH), lambda h: (0, 0, 0))
     shape = jax.ShapeDtypeStruct(query.shape, BF)
-    flops = 2 * count * stretches * 18 * C * C * C
+    square = jax.ShapeDtypeStruct((heads, DH, DH), BF)
     return pl.pallas_call(
-        functools.partial(local_kernel, first_head, stretches, len(partial)),
-        grid=(count,),
-        in_specs=[column] * 4 + [whole] + [pl.BlockSpec(memory_space=pl.ANY)] * len(partial),
-        out_specs=[column] * 4 + [whole],
-        out_shape=[shape] * 4 + [jax.ShapeDtypeStruct(weights.shape, F32)],
-        scratch_shapes=[pltpu.VMEM(weights.shape, F32)],
-        input_output_aliases={5 + i: i for i in range(len(partial))},
-        compiler_params=pltpu.CompilerParams(vmem_limit_bytes=VMEM_LIMIT),
-        cost_estimate=pl.CostEstimate(
-            flops=flops * 8, bytes_accessed=count * tokens * DH * 16, transcendentals=0
+        functools.partial(local_kernel, stretches, exchange),
+        grid=(heads,),
+        in_specs=[column] * 4 + [whole] + [squares] * (cross_bits + 1),
+        out_specs=[column] * 4 + [whole] + [squares] * (cross_bits + 1),
+        out_shape=[shape] * 4
+        + [jax.ShapeDtypeStruct(weights.shape, F32)]
+        + [square] * (cross_bits + 1),
+        scratch_shapes=[pltpu.VMEM(weights.shape, F32)] + exchange.scratch(),
+        compiler_params=pltpu.CompilerParams(
+            vmem_limit_bytes=VMEM_LIMIT, collective_id=0, has_side_effects=True
         ),
         name="local",
-    )(query, key, value, grad_out, weights, *partial)
+    )(query, key, value, grad_out, weights, *sums)
 
 
 def cross_kernel(local_bits, cross_bits, chunks, *refs):
@@ -253,58 +418,19 @@
     )(query, key, value, grad_out, weights, *partial, *gws, *states, adjoint)
 
 
-def exchange(total, products, local_bits):
-    devices = lax.axis_size(AXES)
-    me = lax.axis_index(AXES)
-    cross_bits = devices.bit_length() - 1
-    products = [product for product in products]
-    states = []
-    adjoint = None
-    for i in range(cross_bits):
-        stride = 1 << i
-        pairs = [(p, p ^ stride) for p in range(devices)]
-        if i == cross_bits - 1:
-            pairs = [(p, r) for p, r in pairs if p < r]
-        other = lax.ppermute(total.astype(BF), AXES, pairs).astype(F32)
-        down = [(p, p ^ stride) for p in range(devices) if p & stride]
-        term = level_scale(local_bits + i + 1) * lax.ppermute(
-            products[i].astype(BF), AXES, down
-        ).astype(F32)
-        adjoint = term if adjoint is None else adjoint + term
-        for j in range(i + 1, cross_bits):
-            upper = [(p, p ^ stride) for p in range(devices) if p >> j & 1]
-            products[j] = products[j].astype(F32) + lax.ppermute(
-                products[j].astype(BF), AXES, upper
-            ).astype(F32)
-        reads = me // stride % 2 == 1
-        states.append(
-            jnp.where(reads, level_scale(local_bits + i + 1) * other, 0.0).astype(BF)
-        )
-        total = total.astype(F32) + other
-    return states, adjoint.astype(BF)
-
-
 def shards(query, key, value, grad_out, weights):
     tokens = query.shape[0]
     heads = query.shape[1] // DH
-    stretches = tokens // C
-    local_bits = stretches.bit_length() - 1
+    local_bits = (tokens // C).bit_length() - 1
     cross_bits = LEVELS - 1 - local_bits
-    total, *products = sums_call(
-        query, key, value, grad_out, weights, heads, local_bits, cross_bits
-    )
-    chunks = min(4, heads)
-    count = heads // chunks
-    partial, gws = [], []
-    for c in range(chunks):
-        *partial, gw = local_call(
-            query, key, value, grad_out, weights, partial, c * count, count
-        )
-        gws.append(gw)
-    states, adjoint = exchange(total, products, local_bits)
+    head_bits = lax.axis_size("head").bit_length() - 1
+    sums = sums_call(query, key, value, grad_out, weights, heads, local_bits, cross_bits)
+    outs = local_call(query, key, value, grad_out, weights, sums, head_bits)
+    partial, gw = outs[:4], outs[4]
+    states, adjoint = outs[5 : 5 + cross_bits], outs[5 + cross_bits]
     return tuple(
         cross_call(
-            query, key, value, grad_out, weights, partial, gws, states, adjoint, local_bits
+            query, key, value, grad_out, weights, partial, [gw], states, adjoint, local_bits
         )
     )
 

time: 233 us -> 199 us (0.85)
  Pallas kernels: 109 us -> 183 us
  waiting for transfers between devices: 59.3 us -> 0 us
  starting transfers between devices: 38.6 us -> 0 us
  other arithmetic: 19.8 us -> 0 us
  local copies, waits for them, and re-layouts: 2.79 us -> 14.4 us
    pallas_call x4 -> x1, Pallas kernels: 59.5 us -> 132 us  [local_call(): pl.pallas_call(functools.partial(local_kernel, stretches, exchange), grid...]
    ppermute x14 -> x0, waiting for transfers between devices: 59.3 us -> none  [the longest x4 51.5 us: exchange(): other = lax.ppermute(total.astype(BF), AXES, pairs).astype(F32)]
    ppermute x14 -> x0, starting transfers between devices: 38.6 us -> none  [the longest x6 20.4 us: exchange(): lax.ppermute(products[j].astype(BF), AXES, upper).astype(F32)]
    convert_element_type x11 -> x0, other arithmetic: 19.8 us -> none  [the longest x3 6.49 us: exchange(): products[i].astype(BF)]
    unnamed x16 -> x10, local copies, waits for them, and re-layouts: 2.79 us -> 14.4 us
  transfers between devices with their start and end apart: 14 -> 0, of which waited for: 3 -> 0; matrix products, arithmetic and copies ran while one was open for 7% -> 0% of each run, Pallas kernels for 26% -> 0%
where the time goes in v2:
time: 199 us; the launch traced here: 198 us
  Pallas kernels  183 us (92%)
  local copies, waits for them, and re-layouts  14.4 us (7%)
    pallas_call x1, Pallas kernels, local_call(): pl.pallas_call(functools.partial(local_kernel, stretches, exchange), grid...  132 us
    pallas_call x1, Pallas kernels, cross_call(): pl.pallas_call(functools.partial(cross_kernel, local_bits, cross_bits, le...  31.8 us
    pallas_call x1, Pallas kernels, sums_call(): pl.pallas_call(functools.partial(sums_kernel, local_bits), grid=(heads,),...  18.9 us
    unnamed x10, local copies, waits for them, and re-layouts  14.4 us

profile of v2, /device:TPU:3, one launch (start us, length us, event | category | flops | bytes accessed | tf_op | source)
XLA Modules:
  0.0 197.6 jit_solution(16130830518491215160)
XLA Ops:
  0.6 18.9 %sums.1 = (bf16[16,128,128]{2,1,0:T(8,128)(2,1)}, bf16[16,128,128]{2,1,0:T(8,128)(2,1)}, bf16[16,128,128]{2,1,0:T(8,128)(2,1)}, bf16[16,128,128]{2,1,0:T(8,128)(2,1)}, bf16[16,128,128]{2,1,0:T(8,128)(2,1)}) custom-call(bf16[1024,2048]{1,0:T(8,128)(2,1)} %refs_0_.3, bf16[1024,2048]{1,0:T(8,128)(2,1)} %refs_1_.3, bf16[1024,2048]{1,0:T(8,128)(2,1)} %refs_2_.3, ...), custom_call_target="tpu_custom_call" | custom-call | tf_op jit(solution)/shard_map/sums/pallas_call | solution.py:70
  19.5 131.8 %local.1 = (bf16[1024,2048]{1,0:T(8,128)(2,1)}, bf16[1024,2048]{1,0:T(8,128)(2,1)}, bf16[1024,2048]{1,0:T(8,128)(2,1)}, bf16[1024,2048]{1,0:T(8,128)(2,1)}, f32[...) custom-call(bf16[1024,2048]{1,0:T(8,128)(2,1)} %refs_0_.3, ...), custom_call_target="tpu_custom_call" | custom-call | tf_op jit(solution)/shard_map/local/pallas_call | solution.py:332
  151.4 31.8 %cross.1 = (bf16[1024,2048]{1,0:T(8,128)(2,1)}, bf16[1024,2048]{1,0:T(8,128)(2,1)}, bf16[1024,2048]{1,0:T(8,128)(2,1)}, bf16[1024,2048]{1,0:T(8,128)(2,1)}, bf16[1024,128]{1,0:T(8,128)(2,1)}) custom-call(bf16[1024,2048]{1,0:T(8,128)(2,1)} %refs_0_.3, ...), custom_call_target="tpu_custom_call", output_to_operand_aliasing={{0}: (5, {}), {1}: (6, {}), {2}: (7, {}), {3}: (8, {})} | custom-call | tf_op jit(solution)/shard_map/cross/pallas_call | solution.py:403
  183.2 0.0 copy-start
  183.2 4.9 %copy.22 = bf16[1024,2048]{1,0:T(8,128)(2,1)} copy(bf16[1024,2048]{1,0:T(8,128)(2,1)} %get-tuple-element.40) | data formatting | bytes 8388608
  188.1 0.0 copy-done
  188.1 0.0 copy-start.1
  188.1 2.1 %copy.23 = bf16[1024,2048]{1,0:T(8,128)(2,1)} copy(bf16[1024,2048]{1,0:T(8,128)(2,1)S(1)} %copy-done) | data formatting | bytes 8388608
  190.3 1.6 copy-done.1
  191.8 0.0 copy-start.2
  191.8 2.1 %copy.24 = bf16[1024,2048]{1,0:T(8,128)(2,1)} copy(bf16[1024,2048]{1,0:T(8,128)(2,1)S(1)} %copy-done.1) | data formatting | bytes 8388608
  194.0 1.6 copy-done.2
  195.5 2.0 %copy.25 = bf16[1024,2048]{1,0:T(8,128)(2,1)} copy(bf16[1024,2048]{1,0:T(8,128)(2,1)S(1)} %copy-done.2) | data formatting | bytes 8388608
Async XLA Ops:
  183.2 5.0 %copy-start = (bf16[1024,2048]{1,0:T(8,128)(2,1)S(1)}, bf16[1024,2048]{1,0:T(8,128)(2,1)}, u32[]{:S(2)}) copy-start(bf16[1024,2048]{1,0:T(8,128)(2,1)} %get-tuple-element.41) | copy-start | bytes 12582916
  188.1 3.7 %copy-start.1 = (bf16[1024,2048]{1,0:T(8,128)(2,1)S(1)}, bf16[1024,2048]{1,0:T(8,128)(2,1)}, u32[]{:S(2)}) copy-start(bf16[1024,2048]{1,0:T(8,128)(2,1)} %get-tuple-element.42) | copy-start | bytes 12582916
  191.8 3.7 %copy-start.2 = (bf16[1024,2048]{1,0:T(8,128)(2,1)S(1)}, bf16[1024,2048]{1,0:T(8,128)(2,1)}, u32[]{:S(2)}) copy-start(bf16[1024,2048]{1,0:T(8,128)(2,1)} %get-tuple-element.43) | copy-start | bytes 12582916

commit v3 on v2

--- a/solution.py
+++ b/solution.py
@@ -82,149 +82,266 @@
 class Exchange:
     def __init__(self, local_bits, cross_bits, head_bits, heads, chunks):
         self.local_bits, self.cross_bits, self.head_bits = local_bits, cross_bits, head_bits
-        self.chunks, self.count = chunks, heads // chunks
-        self.heads = heads
-        self.received = cross_bits + cross_bits * (cross_bits + 1) // 2
-        self.sent = cross_bits - 1 + cross_bits * (cross_bits - 1) // 2
-        span = heads - chunks - 3
-        last = max(cross_bits - 1, 1)
-        self.offsets = [heads - chunks - (cross_bits - 1 - i) * span // last for i in range(cross_bits)]
+        self.chunks, self.count, self.heads = chunks, heads // chunks, heads
+        self.size = 1 << head_bits
+        low, high = range(head_bits), range(head_bits, cross_bits)
+        self.low, self.high = low, high
+        landing = [("R", i) for i in low] + [("PR", j) for j in high]
+        landing += [("L", i) for i in low] + [("TL", 0)] + [("PL", j) for j in high]
+        landing += [("T", i) for i in high] + [(("P", j), i) for j in high for i in high if i <= j]
+        sending = [("TR", 0)] + [("PR", j) for j in high]
+        sending += [("L", i) for i in low] + [("TL", 0)] + [("PL", j) for j in high]
+        sending += [("T", i) for i in high] + [(("P", j), i) for j in high for i in high if i <= j]
+        self.lands = {key: n for n, key in enumerate(landing)}
+        self.sends = {key: n for n, key in enumerate(sending)}
+        self.last_time = chunks - 1 + self.size + 1 + 2 * (len(high) - 1)
 
     def scratch(self):
-        sems = pltpu.SemaphoreType.DMA((self.received, self.chunks))
+        sems = pltpu.SemaphoreType.DMA((len(self.lands), self.chunks))
         return [
-            pltpu.VMEM((self.received, self.heads, DH, DH), BF),
-            pltpu.VMEM((max(self.sent, 1), self.heads, DH, DH), BF),
+            pltpu.VMEM((len(self.lands), self.heads, DH, DH), BF),
+            pltpu.VMEM((len(self.sends), self.heads, DH, DH), BF),
             pltpu.VMEM((self.heads, DH, DH), F32),
             sems,
             sems,
         ]
 
     def bind(self, sources, states, adjoint, scratch):
-        self.sources, self.states, self.adjoint = sources, states, adjoint
-        self.landing, self.sending, self.total, self.send_sem, self.recv_sem = scratch
-        head, seq = lax.axis_index("head"), lax.axis_index("seq")
-        self.bits, self.partners = [], []
+        self.total, self.products = sources[0], sources[1:]
+        self.states, self.adjoint = states, adjoint
+        self.landing, self.sending, self.sum, self.send_sem, self.recv_sem = scratch
+        self.z, seq = lax.axis_index("head"), lax.axis_index("seq")
+        self.bit = []
         for i in range(self.cross_bits):
-            name, position, stride = "head", head, 1 << i
+            position, stride = self.z, 1 << i
             if i >= self.head_bits:
-                name, position, stride = "seq", seq, 1 << (i - self.head_bits)
-            bit = (position // stride) % 2
-            self.bits.append(bit)
-            self.partners.append({name: position + (1 - 2 * bit) * stride})
-
-    def slot(self, item, i):
-        return i if item == 0 else self.cross_bits + (item - 1) * item // 2 + i
-
-    def source(self, item, i):
-        if i == 0:
-            return self.sources[item]
-        j = item - 1
-        return self.sending.at[i - 1 if item == 0 else self.cross_bits - 1 + j * (j - 1) // 2 + i - 1]
-
-    def items(self, i):
-        last = i == self.cross_bits - 1
-        set_here, clear_here = self.bits[i] == 1, self.bits[i] == 0
-        yield (0, clear_here, set_here) if last else (0, None, None)
-        yield i + 1, set_here, clear_here
-        for j in range(i + 1, self.cross_bits):
-            yield j + 1, self.bits[j] == 1, self.bits[j] == 1
-
-    def copy(self, item, i, chunk):
-        part = pl.ds(chunk * self.count, self.count)
-        slot = self.slot(item, i)
+                position, stride = seq, 1 << (i - self.head_bits)
+            self.bit.append((position // stride) % 2)
+        self.partner = {
+            i: {"seq": seq + (1 - 2 * self.bit[i]) * (1 << (i - self.head_bits))}
+            for i in self.high
+        }
+        self.right, self.left = {"head": self.z + 1}, {"head": self.z - 1}
+        self.has_right, self.has_left = self.z < self.size - 1, self.z > 0
+
+    def part(self, chunk):
+        return pl.ds(chunk * self.count, self.count)
+
+    def landed(self, key, chunk):
+        return self.landing[self.lands[key], self.part(chunk)].astype(F32)
+
+    def store(self, key, chunk, value):
+        self.sending[self.sends[key], self.part(chunk)] = value.astype(BF)
+
+    def copy(self, key, chunk, device, source=None):
+        slot = self.lands[key]
+        if source is None:
+            source = self.sending.at[self.sends[key]]
         return pltpu.make_async_remote_copy(
-            src_ref=self.source(item, i).at[part],
-            dst_ref=self.landing.at[slot, part],
+            src_ref=source.at[self.part(chunk)],
+            dst_ref=self.landing.at[slot, self.part(chunk)],
             send_sem=self.send_sem.at[slot, chunk],
             recv_sem=self.recv_sem.at[slot, chunk],
-            device_id=self.partners[i],
+            device_id=device,
             device_id_type=pl.DeviceIdType.MESH,
         )
 
-    def when(self, condition, body):
-        if condition is None:
-            body()
-        else:
-            pl.when(condition)(body)
-
-    def start(self, i, chunk):
-        for item, sends, _ in self.items(i):
-            self.when(sends, lambda item=item: self.copy(item, i, chunk).start())
+    def transfers(self):
+        for i in self.low:
+            yield ("R", i), self.right, self.has_right & (((self.z + 1) >> i) % 2 == 1), self.bit[i] == 1
+        for j in self.high:
+            own = self.bit[j] == 1
+            yield ("PR", j), self.right, self.has_right & own, self.has_left & own
+        for i in self.low:
+            block = self.z % (2 << i)
+            yield ("L", i), self.left, block != 0, block != (2 << i) - 1
+        yield ("TL", 0), self.left, self.has_left, self.has_right
+        for j in self.high:
+            own = self.bit[j] == 1
+            yield ("PL", j), self.left, self.has_left & own, self.has_right & own
+        for i in self.high:
+            up, down, always = self.bit[i] == 1, self.bit[i] == 0, self.bit[i] >= 0
+            last = i == self.cross_bits - 1
+            yield ("T", i), self.partner[i], (down if last else always), (up if last else always)
+            yield (("P", i), i), self.partner[i], up, down
+            for j in range(i + 1, self.cross_bits):
+                own = self.bit[j] == 1
+                yield (("P", j), i), self.partner[i], own, own
 
     def greet(self):
         barrier = pltpu.get_barrier_semaphore()
-        for partner in self.partners:
+
+        def signal(device):
             pl.semaphore_signal(
-                barrier, inc=1, device_id=partner, device_id_type=pl.DeviceIdType.MESH
+                barrier, inc=1, device_id=device, device_id_type=pl.DeviceIdType.MESH
             )
-        pl.semaphore_wait(barrier, self.cross_bits)
+
+        for i in self.high:
+            signal(self.partner[i])
+        signal({"head": lax.rem(self.z + 1, self.size)})
+        signal({"head": lax.rem(self.z + self.size - 1, self.size)})
+        pl.semaphore_wait(barrier, len(self.high) + 2)
+
+    def wait(self, chunk, kinds):
+        for key, device, _, receives in self.transfers():
+            if key in kinds:
+                own = self.landing.at[self.lands[key]]
+                pl.when(receives)(
+                    lambda k=key, d=device, r=own: self.copy(k, chunk, d, r).wait_recv()
+                )
+
+    def start(self, chunk, kinds):
+        for key, device, sends, _ in self.transfers():
+            if key in kinds:
+                pl.when(sends)(lambda k=key, d=device: self.copy(k, chunk, d).start())
+
+    def chain(self, key, chunk, own, receives):
+        @pl.when(receives)
+        def _():
+            self.store(key, chunk, own.astype(F32) + self.landed(key, chunk))
+
+        @pl.when(jnp.logical_not(receives))
+        def _():
+            self.store(key, chunk, own)
+
+    def rightward(self, chunk):
+        part = self.part(chunk)
+        self.wait(chunk, [("R", i) for i in self.low] + [("PR", j) for j in self.high])
+        for i in self.low:
+            @pl.when(self.z % (2 << i) == (1 << i) - 1)
+            def _(i=i):
+                value = self.total[part].astype(F32)
+                for k in range(i):
+                    value = value + self.landed(("R", k), chunk)
+                self.store(("TR", 0), chunk, value)
+                self.copy(
+                    ("R", i), chunk, self.right, self.sending.at[self.sends["TR", 0]]
+                ).start()
+
+            @pl.when((self.bit[i] == 1) & (self.z % (1 << i) != (1 << i) - 1))
+            def _(i=i):
+                self.copy(
+                    ("R", i), chunk, self.right, self.landing.at[self.lands["R", i]]
+                ).start()
+
+        for j in self.high:
+
+            @pl.when((self.bit[j] == 1) & self.has_right)
+            def _(j=j):
+                self.chain(("PR", j), chunk, self.products[j][part], self.has_left)
+
+        self.start(chunk, [("PR", j) for j in self.high])
+
+    def leftward(self, chunk):
+        part = self.part(chunk)
+        keys = [("L", i) for i in self.low] + [("TL", 0)] + [("PL", j) for j in self.high]
+        self.wait(chunk, keys)
+        for i in self.low:
+            block = self.z % (2 << i)
+
+            @pl.when(self.bit[i] == 1)
+            def _(i=i, block=block):
+                self.chain(("L", i), chunk, self.products[i][part], block != (2 << i) - 1)
+                self.copy(("L", i), chunk, self.left).start()
+
+            @pl.when((self.bit[i] == 0) & (block != 0))
+            def _(i=i):
+                self.copy(("L", i), chunk, self.left, self.landing.at[self.lands["L", i]]).start()
+
+        @pl.when(self.has_left)
+        def _():
+            self.chain(("TL", 0), chunk, self.total[part], self.has_right)
+
+        for j in self.high:
+
+            @pl.when((self.bit[j] == 1) & self.has_left)
+            def _(j=j):
+                self.chain(("PL", j), chunk, self.products[j][part], self.has_right)
+
+        self.start(chunk, [("TL", 0)] + [("PL", j) for j in self.high])
+
+    def add(self, key, chunk, source, receives, first=None):
+        @pl.when(receives)
+        def _():
+            base = self.sending[self.sends[first or key], self.part(chunk)].astype(F32)
+            self.store(key, chunk, base + self.landed(source, chunk))
+
+    def read(self, i, chunk, state, term):
+        part = self.part(chunk)
+        factor = level_scale(self.local_bits + i + 1)
+
+        @pl.when(self.bit[i] == 1)
+        def _():
+            self.states[i][part] = (factor * self.landed(state, chunk)).astype(BF)
+
+        @pl.when(self.bit[i] == 0)
+        def _():
+            self.states[i][part] = jnp.zeros((self.count, DH, DH), BF)
+            self.sum[part] += factor * self.landed(term, chunk)
+
+    def cross(self, chunk):
+        part = self.part(chunk)
+        self.sum[part] = jnp.zeros((self.count, DH, DH), F32)
+        for i in self.low:
+            self.read(i, chunk, ("R", i), ("L", i))
+        first = self.head_bits
+        value = self.total[part].astype(F32)
+        for i in self.low:
+            value = value + jnp.where(self.bit[i] == 1, self.landed(("R", i), chunk), 0.0)
+        value = value + jnp.where(self.has_right, self.landed(("TL", 0), chunk), 0.0)
+        self.store(("T", first), chunk, value)
+        for j in self.high:
+
+            @pl.when(self.bit[j] == 1)
+            def _(j=j):
+                value = self.products[j][part].astype(F32)
+                value = value + jnp.where(self.has_left, self.landed(("PR", j), chunk), 0.0)
+                value = value + jnp.where(self.has_right, self.landed(("PL", j), chunk), 0.0)
+                self.store((("P", j), first), chunk, value)
+
+        self.start(chunk, [("T", first)] + [(("P", j), first) for j in self.high])
+
+    def arrive(self, i, chunk):
+        part = self.part(chunk)
+        above = range(i + 1, self.cross_bits)
+        self.wait(chunk, [("T", i), (("P", i), i)] + [(("P", j), i) for j in above])
+        if len(above):
+            self.add(("T", i + 1), chunk, ("T", i), self.bit[i] >= 0, ("T", i))
+            for j in above:
+                self.add((("P", j), i + 1), chunk, (("P", j), i), self.bit[j] == 1, (("P", j), i))
+            self.start(chunk, [("T", i + 1)] + [(("P", j), i + 1) for j in above])
+        self.read(i, chunk, ("T", i), (("P", i), i))
+        if not len(above):
+            self.adjoint[part] = self.sum[part].astype(BF)
+
+    def advance(self, time):
+        def at(offset, event):
+            chunk = time - offset
+
+            @pl.when((chunk >= 0) & (chunk < self.chunks))
+            def _():
+                event(chunk)
+
+        at(self.z, self.rightward)
+        at(self.size - 1 - self.z, self.leftward)
+        at(self.size - 1, self.cross)
+        for i in self.high:
+            at(self.size + 1 + 2 * (i - self.head_bits), functools.partial(self.arrive, i))
+
+    def finish(self, steps):
+        def late(time, carry):
+            self.advance(time)
+            return carry
+
+        if self.last_time >= steps:
+            lax.fori_loop(steps, self.last_time + 1, late, 0)
 
         def body(chunk, carry):
-            self.start(0, chunk)
-            return carry
-
-        lax.fori_loop(0, self.chunks, body, 0)
-
-    def arrive(self, i, chunk):
-        part = pl.ds(chunk * self.count, self.count)
-        shape = (self.count, DH, DH)
-        factor = level_scale(self.local_bits + i + 1)
-        last = i == self.cross_bits - 1
-
-        def landed(item):
-            return self.landing[self.slot(item, i), part].astype(F32)
-
-        def add(item):
-            self.source(item, i + 1)[part] = (
-                self.source(item, i)[part].astype(F32) + landed(item)
-            ).astype(BF)
-
-        for item, _, receives in self.items(i):
-            self.when(receives, lambda item=item: self.copy(item, i, chunk).wait_recv())
-            if item == 0:
-                if not last:
-                    add(0)
-            elif item == i + 1:
-                continue
-            else:
-                self.when(receives, lambda item=item: add(item))
-        if not last:
-            self.start(i + 1, chunk)
-
-        @pl.when(self.bits[i] == 1)
-        def _():
-            self.states[i][part] = (factor * landed(0)).astype(BF)
-            if i == 0:
-                self.total[part] = jnp.zeros(shape, F32)
-
-        @pl.when(self.bits[i] == 0)
-        def _():
-            self.states[i][part] = jnp.zeros(shape, BF)
-            if i == 0:
-                self.total[part] = factor * landed(i + 1)
-            else:
-                self.total[part] += factor * landed(i + 1)
-
-        if last:
-            self.adjoint[part] = self.total[part].astype(BF)
-
-    def advance(self, step):
-        pl.when(step == 0)(self.greet)
-        for i in reversed(range(self.cross_bits)):
-            chunk = step - self.offsets[i]
-
-            @pl.when((chunk >= 0) & (chunk < self.chunks))
-            def _(i=i, chunk=chunk):
-                self.arrive(i, chunk)
-
-    def finish(self):
-        def body(chunk, carry):
-            for i in range(self.cross_bits):
-                for item, sends, _ in self.items(i):
-                    self.when(
-                        sends, lambda item=item, i=i: self.copy(item, i, chunk).wait_send()
-                    )
+            for key, device, sends, _ in self.transfers():
+                source = self.landing.at[self.lands[key]]
+                pl.when(sends)(
+                    lambda k=key, d=device, r=source: self.copy(k, chunk, d, r).wait_send()
+                )
             return carry
 
         lax.fori_loop(0, self.chunks, body, 0)
@@ -248,6 +365,7 @@
     def _():
         gw_ref[...] = jnp.zeros_like(gw_ref)
 
+    pl.when(step == 0)(exchange.greet)
     exchange.advance(step)
     wr[...] = head_weights(w_ref, head)
 
@@ -315,7 +433,7 @@
 
     @pl.when(step == pl.num_programs(0) - 1)
     def _():
-        exchange.finish()
+        exchange.finish(exchange.heads)
 
 
 def local_call(query, key, value, grad_out, weights, sums, head_bits):
@@ -323,7 +441,7 @@
     stretches = tokens // C
     heads = query.shape[1] // DH
     cross_bits = len(sums) - 1
-    exchange = Exchange(stretches.bit_length() - 1, cross_bits, head_bits, heads, 4)
+    exchange = Exchange(stretches.bit_length() - 1, cross_bits, head_bits, heads, heads // 2)
     column = pl.BlockSpec((tokens, DH), lambda h: (0, h))
     whole = pl.BlockSpec(weights.shape, lambda h: (0, 0))
     squares = pl.BlockSpec((heads, DH, DH), lambda h: (0, 0, 0))
@@ -412,7 +530,6 @@
         out_shape=[jax.ShapeDtypeStruct(query.shape, BF)] * 4
         + [jax.ShapeDtypeStruct(weights.shape, BF)],
         scratch_shapes=[pltpu.VMEM(weights.shape, F32), pltpu.VMEM(weights.shape, F32)],
-        input_output_aliases={5 + i: i for i in range(4)},
         compiler_params=pltpu.CompilerParams(vmem_limit_bytes=VMEM_LIMIT),
         name="cross",
     )(query, key, value, grad_out, weights, *partial, *gws, *states, adjoint)

time: 199 us -> 150 us (0.75)
  Pallas kernels: 183 us -> 148 us
  local copies, waits for them, and re-layouts: 14.4 us -> 0 us
    pallas_call x1, Pallas kernels: 132 us -> 97.3 us  [local_call(): pl.pallas_call(functools.partial(local_kernel, stretches, exchange), grid...]
    unnamed x10 -> x0, local copies, waits for them, and re-layouts: 14.4 us -> none
where the time goes in v3:
time: 150 us; the launch traced here: 149 us
  Pallas kernels  148 us (99%)
    pallas_call x1, Pallas kernels, local_call(): pl.pallas_call(functools.partial(local_kernel, stretches, exchange), grid...  97.3 us
    pallas_call x1, Pallas kernels, cross_call(): pl.pallas_call(functools.partial(cross_kernel, local_bits, cross_bits, le...  31.8 us
    pallas_call x1, Pallas kernels, sums_call(): pl.pallas_call(functools.partial(sums_kernel, local_bits), grid=(heads,),...  18.9 us

profile of v3, /device:TPU:3, one launch (start us, length us, event | category | flops | bytes accessed | tf_op | source)
XLA Modules:
  0.0 148.7 jit_solution(11674142606465216527)
XLA Ops:
  0.6 18.9 %sums.1 = (bf16[16,128,128]{2,1,0:T(8,128)(2,1)}, bf16[16,128,128]{2,1,0:T(8,128)(2,1)}, bf16[16,128,128]{2,1,0:T(8,128)(2,1)}, bf16[16,128,128]{2,1,0:T(8,128)(2,1)}, bf16[16,128,128]{2,1,0:T(8,128)(2,1)}) custom-call(bf16[1024,2048]{1,0:T(8,128)(2,1)} %refs_0_.3, bf16[1024,2048]{1,0:T(8,128)(2,1)} %refs_1_.3, bf16[1024,2048]{1,0:T(8,128)(2,1)} %refs_2_.3, ...), custom_call_target="tpu_custom_call" | custom-call | tf_op jit(solution)/shard_map/sums/pallas_call | solution.py:70
  19.5 97.3 %local.1 = (bf16[1024,2048]{1,0:T(8,128)(2,1)}, bf16[1024,2048]{1,0:T(8,128)(2,1)}, bf16[1024,2048]{1,0:T(8,128)(2,1)}, bf16[1024,2048]{1,0:T(8,128)(2,1)}, f32[...) custom-call(bf16[1024,2048]{1,0:T(8,128)(2,1)} %refs_0_.3, ...), custom_call_target="tpu_custom_call" | custom-call | tf_op jit(solution)/shard_map/local/pallas_call | solution.py:450
  116.9 31.8 %cross.1 = (bf16[1024,2048]{1,0:T(8,128)(2,1)}, bf16[1024,2048]{1,0:T(8,128)(2,1)}, bf16[1024,2048]{1,0:T(8,128)(2,1)}, bf16[1024,2048]{1,0:T(8,128)(2,1)}, bf16[1024,128]{1,0:T(8,128)(2,1)}) custom-call(bf16[1024,2048]{1,0:T(8,128)(2,1)} %refs_0_.3, bf16[1024,2048]{1,0:T(8,128)(2,1)} %refs_1_.3, bf16[1024,2048]{1,0:T(8,128)(2,1)} %refs_2_.3, ...), custom_call_target="tpu_custom_call" | custom-call | tf_op jit(solution)/shard_map/cross/pallas_call | solution.py:521
